TPU v7x, 128 devices: a whole 4x4x4 slice. The times are simulated.
128 devices in a mesh: walk: 16 (over x, y_lo, core), chol: 8 (over z, y_hi).
Axes of the slice: x: 4, y: 4 (y_hi: 2, y_lo: 2; y = y_hi * 2 + y_lo), z: 4, core: 2. Of those that a mesh axis runs over, the one named last changes fastest.
Arguments:
- orbitals: float32 [256, 32, 512], P(('walk', 'chol')), may hold values from -3 to 3
- dest: int32 [256, 2], P(('walk', 'chol')), may hold values from -1 to 15, as said below
- chol_vectors: bfloat16 [2048, 32, 512], P('chol'), may hold values from -2 to 2
Outputs:
- energy: float32 [512], P(('walk', 'chol'))
- force_bias: float32 [512, 2048], P(('walk', 'chol'))
- log_correlation: float32 [512], P(('walk', 'chol'))
Inputs may be any that keep to these rules, and one draw needn't show every extreme that they name: `dest`: entry (r, k) names the walk index that receives copy k of walker r, or -1 where that copy is not made. Among the devices that share a chol index, each device sends exactly 2 copies, at most one of them to any walk index; half of the walk indices receive exactly 4 copies and the others none.
All inputs are finite; a program needn't handle non-finite values.
Results may differ from a plain program's by a relative error of at most 0.0029.
Values may be sent and summed in bfloat16 or wider, within the bound.
No kernel may reach another device: no remote copies, remote signals or barrier semaphores. Data moves between devices by JAX's collectives and lax.ppermute only.
A program may use at most 128 MiB of HBM per device.

v0:
```python
import math

import jax
import jax.numpy as jnp
from jax import lax
from jax.sharding import PartitionSpec as P


def from_behind(value, axis, by):
    peers = lax.axis_size(axis)
    return lax.ppermute(value, axis, [(i, (i + by) % peers) for i in range(peers)])


def correlation_green(walkers):
    elec = walkers.shape[1]
    square = walkers[:, :, :elec]
    gram = jnp.einsum("wba,wbc->wac", square, square, precision=lax.Precision.HIGHEST)
    rotated = jnp.einsum("wba,wbm->wam", square, walkers, precision=lax.Precision.HIGHEST)
    factor = jnp.linalg.cholesky(gram)
    middle = lax.linalg.triangular_solve(factor, rotated, left_side=True, lower=True)
    green = lax.linalg.triangular_solve(
        factor, middle, left_side=True, lower=True, transpose_a=True
    )
    diagonal = jnp.diagonal(factor, axis1=1, axis2=2)
    log_correlation = jnp.sum(jnp.log(diagonal), axis=1) / elec
    return (green.astype(jnp.bfloat16), log_correlation)


def stop_terms(vectors, block, weight):
    count, elec, basis = vectors.shape
    walkers = block.shape[0]
    group_size = math.gcd(count, 32)
    grouped = vectors.reshape(count // group_size, group_size * elec, basis)
    flat_block = block.reshape(walkers * elec, basis)

    def one_group(group):
        product = lax.dot_general(
            group, flat_block, (((1,), (1,)), ((), ())), preferred_element_type=jnp.float32
        )
        product = product.reshape(group_size, elec, walkers, elec)
        values = jnp.sum(jnp.diagonal(product, axis1=1, axis2=3), axis=2).T
        crossed = jnp.einsum("giwj,gjwi->wg", product, product)
        return (values, jnp.sum(2.0 * values * values - crossed, axis=1))

    values, parts = lax.map(one_group, grouped)
    values = values.transpose(1, 0, 2).reshape(walkers, count)
    return (values, jnp.sum(parts, axis=0) * weight)


def body(orbitals, dest, chol_vectors):
    walk_count = lax.axis_size("walk")
    walk_dev, elec, basis = orbitals.shape
    slots = 2 * walk_dev
    entries = dest.reshape(-1)
    entry_ids = jnp.arange(entries.shape[0], dtype=jnp.int32)
    targets = jnp.arange(walk_count, dtype=jnp.int32)
    match = entries[None, :] == targets[:, None]
    chosen = jnp.sum(jnp.where(match, entry_ids[None, :], 0), axis=1)
    present = jnp.any(match, axis=1)
    outgoing = jnp.where(present[:, None, None], orbitals[chosen // 2], 0.0)
    flags = present.astype(jnp.float32)
    arrived, arrived_flags = (
        lax.all_to_all(outgoing, "walk", split_axis=0, concat_axis=0, tiled=True),
        lax.all_to_all(flags, "walk", split_axis=0, concat_axis=0, tiled=True),
    )
    live = arrived_flags > 0.5
    live_count = live.astype(jnp.int32)
    before = jnp.cumsum(live_count) - live_count
    slot_ids = jnp.arange(slots, dtype=jnp.int32)
    pick = live[None, :] & (before[None, :] == slot_ids[:, None])
    source = jnp.sum(jnp.where(pick, targets[None, :], 0), axis=1)
    filled = jnp.any(pick, axis=1)
    trial = jnp.eye(elec, basis, dtype=jnp.float32)
    walkers = jnp.where(filled[:, None, None], arrived[source], trial[None])
    green, log_correlation = correlation_green(walkers)
    chol_count = lax.axis_size("chol")
    position = lax.axis_index("chol")
    local = chol_vectors.shape[0]
    total = chol_count * local
    weight = 1.0 / (elec * total)

    def pass_green(block):
        return from_behind(block, "chol", 1)

    def pass_tallies(tallies):
        return from_behind(tallies, "chol", 1)

    def add_stop(tallies, block):
        values, parts = stop_terms(chol_vectors, block, weight)
        bias_tally = lax.dynamic_update_slice(tallies[0], values, (0, position * local))
        return (bias_tally, tallies[1] + parts)

    start = (jnp.zeros((slots, total), jnp.float32), jnp.zeros((slots,), jnp.float32))
    tallies = add_stop(start, green)

    def advance(index, carry):
        block, tallies = carry
        block = pass_green(block)
        tallies = pass_tallies(tallies)
        return (block, add_stop(tallies, block))

    block, tallies = lax.fori_loop(1, chol_count, advance, (green, tallies))
    bias, energy = pass_tallies(tallies)
    weights_mask = filled.astype(jnp.float32)
    return (energy * weights_mask, bias * weights_mask[:, None], log_correlation * weights_mask)


def solution(mesh):
    placed = (P(("walk", "chol"), None, None), P(("walk", "chol"), None), P("chol", None, None))
    return jax.shard_map(
        body,
        mesh=mesh,
        in_specs=placed,
        out_specs=(P(("walk", "chol")), P(("walk", "chol"), None), P(("walk", "chol"))),
        check_vma=False,
    )
```

profile of v0, /device:TPU:1, one launch (start us, length us, event | category | flops | bytes accessed | tf_op | source)
XLA Modules:
  0.0 814.0 jit_solution(16109957207982822518)
XLA Ops:
  2.2 6.8 all-to-all-start
  11.5 3.0 all-to-all-done
  14.5 4.1 all-to-all-start.1
  19.9 14.2 %all-to-all-done.1 = f32[16,32,512]{2,1,0:T(8,128)S(1)} async-done(((f32[16,32,512]{2,1,0:T(8,128)}), f32[16,32,512]{2,1,0:T(8,128)S(1)}, u32[]{:S(2)}, u32[]{:S(2)}) %all-to-all-start.1) | async-done | bytes 1048608 | tf_op jit(solution)/shard_map/all_to_all | solution.py:63
  35.7 11.7 %custom-call.9 = f32[4,32,32]{2,1,0:T(8,128)S(1)} custom-call(f32[4,32,32]{2,1,0:T(8,128)S(1)} %fusion.7), custom_call_target="Cholesky" | custom-call | tf_op jit(solution)/shard_map/jit(cholesky)/cholesky | solution.py:19
  48.2 9.8 %custom-call.10 = f32[4,1,32,32]{2,3,1,0:T(8,128)S(1)} custom-call(f32[4,1,32,32]{3,2,1,0:T(8,128)S(1)} %get-tuple-element.171), custom_call_target="InvertDiagBlocksLowerTriangular" | custom-call | tf_op jit(solution)/shard_map/triangular_solve | solution.py:21
  58.9 86.5 %while.48 = (s32[]{:T(128)}, f32[8,4,32]{2,1,0:T(4,128)S(1)}, f32[8,4]{1,0:T(8,128)S(1)}, bf16[8,1024,512]{2,1,0:T(8,128)(2,1)}, bf16[128,512]{1,0:T(8,128)(2,1)S(1)}, /*index=5*/s32[]{:T(128)}, f32[]{:T(128)}, s32[]{:T(128)}) while((s32[]{:T(128)}, f32[8,4,32]{2,1,0:T(4,128)S(1)}, f32[8,4]{1,0:T(8,128)S(1)}, ...), condition=%wide.region_10.11_spmd, body=%wide.region_7.10_spmd.sunk | while | flops 134484352 | bytes 7003669 | solution.py:45
  64.9 2.3 copy.79
  86.5 2.3 copy.79
  119.0 2.3 copy.79
  140.6 2.3 copy.79
  145.6 660.6 %while.50 = (s32[]{:T(128)}, bf16[4,32,512]{2,1,0:T(8,128)(2,1)S(1)}, f32[4,2048]{1,0:T(4,128)S(1)}, f32[4]{0:T(128)S(1)}, bf16[256,32,512]{2,1,0:T(8,128)(2,1)}...) while((s32[]{:T(128)}, ...), condition=%wide.region_18.19_spmd, body=%wide.region_12.18_spmd.sunk | while | flops 134484384 | bytes 8011858 | solution.py:102
  145.6 2.7 collective-permute-start
  150.0 2.6 collective-permute-start.2
  154.6 86.5 %while.51 = (s32[]{:T(128)}, f32[8,4,32]{2,1,0:T(4,128)S(1)}, f32[8,4]{1,0:T(8,128)S(1)}, bf16[8,1024,512]{2,1,0:T(8,128)(2,1)}, bf16[128,512]{1,0:T(8,128)(2,1)S(1)}, /*index=5*/s32[]{:T(128)}, f32[]{:T(128)}, s32[]{:T(128)}) while((s32[]{:T(128)}, f32[8,4,32]{2,1,0:T(4,128)S(1)}, f32[8,4]{1,0:T(8,128)S(1)}, ...), condition=%wide.region_16.16_spmd, body=%wide.region_13.15_spmd.sunk | while | flops 134484352 | bytes 7003669 | solution.py:45
  182.2 2.3 copy.83
  193.0 2.3 copy.83
  203.8 2.3 copy.83
  241.3 2.4 collective-permute-start.1
  245.1 3.7 collective-permute-done
  248.7 86.5 %while.51 = (s32[]{:T(128)}, f32[8,4,32]{2,1,0:T(4,128)S(1)}, f32[8,4]{1,0:T(8,128)S(1)}, bf16[8,1024,512]{2,1,0:T(8,128)(2,1)}, bf16[128,512]{1,0:T(8,128)(2,1)S(1)}, /*index=5*/s32[]{:T(128)}, f32[]{:T(128)}, s32[]{:T(128)}) while((s32[]{:T(128)}, f32[8,4,32]{2,1,0:T(4,128)S(1)}, f32[8,4]{1,0:T(8,128)S(1)}, ...), condition=%wide.region_16.16_spmd, body=%wide.region_13.15_spmd.sunk | while | flops 134484352 | bytes 7003669 | solution.py:45
  338.0 4.9 collective-permute-done
  342.9 86.5 %while.51 = (s32[]{:T(128)}, f32[8,4,32]{2,1,0:T(4,128)S(1)}, f32[8,4]{1,0:T(8,128)S(1)}, bf16[8,1024,512]{2,1,0:T(8,128)(2,1)}, bf16[128,512]{1,0:T(8,128)(2,1)S(1)}, /*index=5*/s32[]{:T(128)}, f32[]{:T(128)}, s32[]{:T(128)}) while((s32[]{:T(128)}, f32[8,4,32]{2,1,0:T(4,128)S(1)}, f32[8,4]{1,0:T(8,128)S(1)}, ...), condition=%wide.region_16.16_spmd, body=%wide.region_13.15_spmd.sunk | while | flops 134484352 | bytes 7003669 | solution.py:45
  431.0 6.1 collective-permute-done
  437.1 86.5 %while.51 = (s32[]{:T(128)}, f32[8,4,32]{2,1,0:T(4,128)S(1)}, f32[8,4]{1,0:T(8,128)S(1)}, bf16[8,1024,512]{2,1,0:T(8,128)(2,1)}, bf16[128,512]{1,0:T(8,128)(2,1)S(1)}, /*index=5*/s32[]{:T(128)}, f32[]{:T(128)}, s32[]{:T(128)}) while((s32[]{:T(128)}, f32[8,4,32]{2,1,0:T(4,128)S(1)}, f32[8,4]{1,0:T(8,128)S(1)}, ...), condition=%wide.region_16.16_spmd, body=%wide.region_13.15_spmd.sunk | while | flops 134484352 | bytes 7003669 | solution.py:45
  524.0 7.2 collective-permute-done
  531.2 86.5 %while.51 = (s32[]{:T(128)}, f32[8,4,32]{2,1,0:T(4,128)S(1)}, f32[8,4]{1,0:T(8,128)S(1)}, bf16[8,1024,512]{2,1,0:T(8,128)(2,1)}, bf16[128,512]{1,0:T(8,128)(2,1)S(1)}, /*index=5*/s32[]{:T(128)}, f32[]{:T(128)}, s32[]{:T(128)}) while((s32[]{:T(128)}, f32[8,4,32]{2,1,0:T(4,128)S(1)}, f32[8,4]{1,0:T(8,128)S(1)}, ...), condition=%wide.region_16.16_spmd, body=%wide.region_13.15_spmd.sunk | while | flops 134484352 | bytes 7003669 | solution.py:45
  618.2 7.2 collective-permute-done
  625.4 86.5 %while.51 = (s32[]{:T(128)}, f32[8,4,32]{2,1,0:T(4,128)S(1)}, f32[8,4]{1,0:T(8,128)S(1)}, bf16[8,1024,512]{2,1,0:T(8,128)(2,1)}, bf16[128,512]{1,0:T(8,128)(2,1)S(1)}, /*index=5*/s32[]{:T(128)}, f32[]{:T(128)}, s32[]{:T(128)}) while((s32[]{:T(128)}, f32[8,4,32]{2,1,0:T(4,128)S(1)}, f32[8,4]{1,0:T(8,128)S(1)}, ...), condition=%wide.region_16.16_spmd, body=%wide.region_13.15_spmd.sunk | while | flops 134484352 | bytes 7003669 | solution.py:45
  712.3 7.2 collective-permute-done
  719.5 86.5 %while.51 = (s32[]{:T(128)}, f32[8,4,32]{2,1,0:T(4,128)S(1)}, f32[8,4]{1,0:T(8,128)S(1)}, bf16[8,1024,512]{2,1,0:T(8,128)(2,1)}, bf16[128,512]{1,0:T(8,128)(2,1)S(1)}, /*index=5*/s32[]{:T(128)}, f32[]{:T(128)}, s32[]{:T(128)}) while((s32[]{:T(128)}, f32[8,4,32]{2,1,0:T(4,128)S(1)}, f32[8,4]{1,0:T(8,128)S(1)}, ...), condition=%wide.region_16.16_spmd, body=%wide.region_13.15_spmd.sunk | while | flops 134484352 | bytes 7003669 | solution.py:45
  807.4 5.3 collective-permute-done.3
  (918 shorter events, 695.4 us)
Async XLA Ops:
  0.6 9.1 %copy-start = (f32[2,32,512]{2,1,0:T(8,128)S(1)}, f32[2,32,512]{2,1,0:T(8,128)}, u32[]{:S(2)}) copy-start(f32[2,32,512]{2,1,0:T(8,128)} %param.9) | copy-start | bytes 393220
  2.2 12.3 %all-to-all-start = ((f32[16,1,1]{2,1,0:T(1,128)}), f32[16,1,1]{2,1,0:T(1,128)S(1)}, u32[]{:S(2)}, u32[]{:S(2)}) async-start(f32[16,1,1]{2,1,0:T(1,128)} %copy.45), calls=%async_computation | async-start | bytes 16384 | tf_op jit(solution)/shard_map/all_to_all | solution.py:64
  14.5 19.7 %all-to-all-start.1 = ((f32[16,32,512]{2,1,0:T(8,128)}), f32[16,32,512]{2,1,0:T(8,128)S(1)}, u32[]{:S(2)}, u32[]{:S(2)}) async-start(f32[16,32,512]{2,1,0:T(8,128)} %broadcast_select_fusion), calls=%async_computation.1 | async-start | bytes 2097152 | tf_op jit(solution)/shard_map/all_to_all | solution.py:63
  19.3 39.6 %copy-start.3 = (pred[4]{0:T(512)(128)(4,1)}, pred[4]{0:T(512)(128)(4,1)S(1)}, u32[]{:S(2)}) copy-start(pred[4]{0:T(512)(128)(4,1)S(1)} %fusion.15) | copy-start | bytes 16
  145.5 660.8 %copy-start.2 = (f32[4,32,32]{2,1,0:T(8,128)S(1)}, f32[4,32,32]{2,1,0:T(8,128)}, u32[]{:S(2)}) copy-start(f32[4,32,32]{2,1,0:T(8,128)} %get-tuple-element.172) | copy-start | bytes 49156
  145.5 661.1 %copy-start.1 = (s32[32]{0:T(128)S(1)}, s32[32]{0:T(128)}, u32[]{:S(2)}) copy-start(s32[32]{0:T(128)} %or_bitcast_fusion.2) | copy-start | bytes 388
  145.5 667.2 %copy-start.4 = (pred[4]{0:T(512)(128)(4,1)S(1)}, pred[4]{0:T(512)(128)(4,1)}, u32[]{:S(2)}) copy-start(pred[4]{0:T(512)(128)(4,1)} %copy-done.3) | copy-start | bytes 16
  145.6 667.7 %copy-start.5 = (f32[4]{0:T(128)S(1)}, f32[4]{0:T(128)}, u32[]{:S(2)}) copy-start(f32[4]{0:T(128)} %convert_element_type.58) | copy-start | bytes 52
  145.6 9.0 %collective-permute-start = (bf16[4,32,512]{2,1,0:T(8,128)(2,1)S(1)}, bf16[4,32,512]{2,1,0:T(8,128)(2,1)S(1)}, u32[]{:S(2)}, u32[]{:S(2)}) collective-permute-start(bf16[4,32,512]{2,1,0:T(8,128)(2,1)S(1)} %get-tuple-element.352), channel_id=1, source_target_pairs={{0,1},{1,2},{2,3},{3,4},{4,5},{5,6},{6,7},{7,0},{8,9},{9,10},{10,1... | collective-permute-start | bytes 393224 | tf_op jit(solution)/shard_map/while/body/eval_jaxpr/ppermute | solution.py:11
  148.3 92.9 %collective-permute-start.1 = (f32[4,2048]{1,0:T(4,128)S(1)}, f32[4,2048]{1,0:T(4,128)S(1)}, u32[]{:S(2)}, u32[]{:S(2)}) collective-permute-start(f32[4,2048]{1,0:T(4,128)S(1)} %get-tuple-element.353), channel_id=1, source_target_pairs={{0,1},{1,2},{2,3},{3,4},{4,5},{5,6},{6,7},{7,0},{8,9},{9,10},{10,1... | collective-permute-start | bytes 98312 | tf_op jit(solution)/shard_map/while/body/eval_jaxpr/ppermute | solution.py:11
  150.0 91.2 %collective-permute-start.2 = (f32[4]{0:T(128)S(1)}, f32[4]{0:T(128)S(1)}, u32[]{:S(2)}, u32[]{:S(2)}) collective-permute-start(f32[4]{0:T(128)S(1)} %get-tuple-element.354), channel_id=1, source_target_pairs={{0,1},{1,2},{2,3},{3,4},{4,5},{5,6},{6,7},{7,0},{8,9},{9,10},{10,1... | collective-permute-start | bytes 56 | tf_op jit(solution)/shard_map/while/body/eval_jaxpr/ppermute | solution.py:11
  241.2 7.5 collective-permute-start
  241.3 94.0 %collective-permute-start.1 = (f32[4,2048]{1,0:T(4,128)S(1)}, f32[4,2048]{1,0:T(4,128)S(1)}, u32[]{:S(2)}, u32[]{:S(2)}) collective-permute-start(f32[4,2048]{1,0:T(4,128)S(1)} %get-tuple-element.353), channel_id=1, source_target_pairs={{0,1},{1,2},{2,3},{3,4},{4,5},{5,6},{6,7},{7,0},{8,9},{9,10},{10,1... | collective-permute-start | bytes 98312 | tf_op jit(solution)/shard_map/while/body/eval_jaxpr/ppermute | solution.py:11
  243.7 91.7 %collective-permute-start.2 = (f32[4]{0:T(128)S(1)}, f32[4]{0:T(128)S(1)}, u32[]{:S(2)}, u32[]{:S(2)}) collective-permute-start(f32[4]{0:T(128)S(1)} %get-tuple-element.354), channel_id=1, source_target_pairs={{0,1},{1,2},{2,3},{3,4},{4,5},{5,6},{6,7},{7,0},{8,9},{9,10},{10,1... | collective-permute-start | bytes 56 | tf_op jit(solution)/shard_map/while/body/eval_jaxpr/ppermute | solution.py:11
  335.4 7.5 collective-permute-start
  335.5 94.0 %collective-permute-start.1 = (f32[4,2048]{1,0:T(4,128)S(1)}, f32[4,2048]{1,0:T(4,128)S(1)}, u32[]{:S(2)}, u32[]{:S(2)}) collective-permute-start(f32[4,2048]{1,0:T(4,128)S(1)} %get-tuple-element.353), channel_id=1, source_target_pairs={{0,1},{1,2},{2,3},{3,4},{4,5},{5,6},{6,7},{7,0},{8,9},{9,10},{10,1... | collective-permute-start | bytes 98312 | tf_op jit(solution)/shard_map/while/body/eval_jaxpr/ppermute | solution.py:11
  336.6 92.9 %collective-permute-start.2 = (f32[4]{0:T(128)S(1)}, f32[4]{0:T(128)S(1)}, u32[]{:S(2)}, u32[]{:S(2)}) collective-permute-start(f32[4]{0:T(128)S(1)} %get-tuple-element.354), channel_id=1, source_target_pairs={{0,1},{1,2},{2,3},{3,4},{4,5},{5,6},{6,7},{7,0},{8,9},{9,10},{10,1... | collective-permute-start | bytes 56 | tf_op jit(solution)/shard_map/while/body/eval_jaxpr/ppermute | solution.py:11
  429.6 7.5 collective-permute-start
  429.6 94.0 %collective-permute-start.1 = (f32[4,2048]{1,0:T(4,128)S(1)}, f32[4,2048]{1,0:T(4,128)S(1)}, u32[]{:S(2)}, u32[]{:S(2)}) collective-permute-start(f32[4,2048]{1,0:T(4,128)S(1)} %get-tuple-element.353), channel_id=1, source_target_pairs={{0,1},{1,2},{2,3},{3,4},{4,5},{5,6},{6,7},{7,0},{8,9},{9,10},{10,1... | collective-permute-start | bytes 98312 | tf_op jit(solution)/shard_map/while/body/eval_jaxpr/ppermute | solution.py:11
  429.7 94.0 %collective-permute-start.2 = (f32[4]{0:T(128)S(1)}, f32[4]{0:T(128)S(1)}, u32[]{:S(2)}, u32[]{:S(2)}) collective-permute-start(f32[4]{0:T(128)S(1)} %get-tuple-element.354), channel_id=1, source_target_pairs={{0,1},{1,2},{2,3},{3,4},{4,5},{5,6},{6,7},{7,0},{8,9},{9,10},{10,1... | collective-permute-start | bytes 56 | tf_op jit(solution)/shard_map/while/body/eval_jaxpr/ppermute | solution.py:11
  523.7 7.5 collective-permute-start
  523.8 94.0 %collective-permute-start.1 = (f32[4,2048]{1,0:T(4,128)S(1)}, f32[4,2048]{1,0:T(4,128)S(1)}, u32[]{:S(2)}, u32[]{:S(2)}) collective-permute-start(f32[4,2048]{1,0:T(4,128)S(1)} %get-tuple-element.353), channel_id=1, source_target_pairs={{0,1},{1,2},{2,3},{3,4},{4,5},{5,6},{6,7},{7,0},{8,9},{9,10},{10,1... | collective-permute-start | bytes 98312 | tf_op jit(solution)/shard_map/while/body/eval_jaxpr/ppermute | solution.py:11
  523.9 94.0 %collective-permute-start.2 = (f32[4]{0:T(128)S(1)}, f32[4]{0:T(128)S(1)}, u32[]{:S(2)}, u32[]{:S(2)}) collective-permute-start(f32[4]{0:T(128)S(1)} %get-tuple-element.354), channel_id=1, source_target_pairs={{0,1},{1,2},{2,3},{3,4},{4,5},{5,6},{6,7},{7,0},{8,9},{9,10},{10,1... | collective-permute-start | bytes 56 | tf_op jit(solution)/shard_map/while/body/eval_jaxpr/ppermute | solution.py:11
  617.9 7.5 collective-permute-start
  618.0 94.0 %collective-permute-start.1 = (f32[4,2048]{1,0:T(4,128)S(1)}, f32[4,2048]{1,0:T(4,128)S(1)}, u32[]{:S(2)}, u32[]{:S(2)}) collective-permute-start(f32[4,2048]{1,0:T(4,128)S(1)} %get-tuple-element.353), channel_id=1, source_target_pairs={{0,1},{1,2},{2,3},{3,4},{4,5},{5,6},{6,7},{7,0},{8,9},{9,10},{10,1... | collective-permute-start | bytes 98312 | tf_op jit(solution)/shard_map/while/body/eval_jaxpr/ppermute | solution.py:11
  618.0 94.0 %collective-permute-start.2 = (f32[4]{0:T(128)S(1)}, f32[4]{0:T(128)S(1)}, u32[]{:S(2)}, u32[]{:S(2)}) collective-permute-start(f32[4]{0:T(128)S(1)} %get-tuple-element.354), channel_id=1, source_target_pairs={{0,1},{1,2},{2,3},{3,4},{4,5},{5,6},{6,7},{7,0},{8,9},{9,10},{10,1... | collective-permute-start | bytes 56 | tf_op jit(solution)/shard_map/while/body/eval_jaxpr/ppermute | solution.py:11
  712.0 7.5 collective-permute-start
  712.1 94.0 %collective-permute-start.1 = (f32[4,2048]{1,0:T(4,128)S(1)}, f32[4,2048]{1,0:T(4,128)S(1)}, u32[]{:S(2)}, u32[]{:S(2)}) collective-permute-start(f32[4,2048]{1,0:T(4,128)S(1)} %get-tuple-element.353), channel_id=1, source_target_pairs={{0,1},{1,2},{2,3},{3,4},{4,5},{5,6},{6,7},{7,0},{8,9},{9,10},{10,1... | collective-permute-start | bytes 98312 | tf_op jit(solution)/shard_map/while/body/eval_jaxpr/ppermute | solution.py:11
  712.2 94.0 %collective-permute-start.2 = (f32[4]{0:T(128)S(1)}, f32[4]{0:T(128)S(1)}, u32[]{:S(2)}, u32[]{:S(2)}) collective-permute-start(f32[4]{0:T(128)S(1)} %get-tuple-element.354), channel_id=1, source_target_pairs={{0,1},{1,2},{2,3},{3,4},{4,5},{5,6},{6,7},{7,0},{8,9},{9,10},{10,1... | collective-permute-start | bytes 56 | tf_op jit(solution)/shard_map/while/body/eval_jaxpr/ppermute | solution.py:11
  806.2 7.1 collective-permute-start.4
  806.3 6.5 collective-permute-start.3
where the time goes:
time: 829 us; the launch traced here: 814 us
  local copies, waits for them, and re-layouts  508 us (61%)
  other arithmetic  168 us (20%)
  waiting for transfers between devices  60.9 us (7%)
  matrix products  47.1 us (6%)
  starting transfers between devices  26.6 us (3%)
    transpose x64, local copies, waits for them, and re-layouts, one_group(): values = jnp.sum(jnp.diagonal(product, axis1=1, axis2=3), axis=2).T  148 us
    gather x64, local copies, waits for them, and re-layouts, one_group(): values = jnp.sum(jnp.diagonal(product, axis1=1, axis2=3), axis=2).T  144 us
    while x64, other arithmetic  130 us
    while x78, local copies, waits for them, and re-layouts  120 us
    dynamic_slice x64, local copies, waits for them, and re-layouts, stop_terms(): values, parts = lax.map(one_group, grouped)  83 us
    dot_general x64, matrix products, one_group(): lax.dot_general(group, flat_block, (((1,), (1,)), ((), ())), preferred_el...  45.6 us
    ppermute x23, waiting for transfers between devices, from_behind(): lax.ppermute(value, axis, [(i, (i + by) % peers) for i in range(peers)])  43.6 us
  transfers between devices with their start and end apart: 25, of which 10 were waited for; matrix products, arithmetic and copies ran while one was open for 75% of the time, Pallas kernels for 0%

commit v1 on v0

v1 whole, which is shorter than its diff:
```python
import functools

import jax
import jax.numpy as jnp
from jax import lax
from jax.experimental import pallas as pl
from jax.experimental.pallas import tpu as pltpu
from jax.sharding import PartitionSpec as P

F32 = jnp.float32
BF16 = jnp.bfloat16
HIGH = lax.Precision.HIGHEST


def iota(shape, axis):
    return lax.broadcasted_iota(jnp.int32, shape, axis)


def green_kernel(dest_ref, walkers_ref, packet_ref, log_ref):
    count, elec, basis = walkers_ref.shape
    work = []
    for r in range(count):
        full = walkers_ref[r]
        work.append(
            lax.dot_general(
                full[:, :elec], full, (((0,), (0,)), ((), ())), precision=HIGH, preferred_element_type=F32
            )
        )
    rows = iota((elec, 1), 0)
    lanes = iota((8, 128), 1)
    pivots = [jnp.ones((1, 128), F32) for _ in range(count)]
    lane = iota((1, 128), 1)
    for k in range(elec):
        for r in range(count):
            a = work[r]
            row = a[k : k + 1, :]
            column = a[:, k : k + 1]
            pivot = row[:, k : k + 1]
            inverse = 1.0 / pivot
            pivots[r] = jnp.where(lane == k, pivot, pivots[r])
            scaled = row * inverse
            work[r] = jnp.where(rows == k, scaled, a - column * scaled)
    out = jnp.zeros((8, 128), F32)
    for r in range(count):
        wanted = (dest_ref[r, 0] >= 0) | (dest_ref[r, 1] >= 0)
        packet_ref[r * elec : (r + 1) * elec, :] = jnp.where(wanted, work[r], 0.0).astype(BF16)
        total = jnp.sum(jnp.where(lane < elec, jnp.log(pivots[r]), 0.0), axis=1, keepdims=True)
        total = jnp.where(wanted, total * (0.5 / elec), 0.0)
        out = jnp.where(lanes == r, total, out)
    log_ref[...] = out
    tag = jnp.full((8, basis), -1.0, F32)
    wide = iota((8, basis), 1)
    for r in range(count):
        for k in range(2):
            tag = jnp.where(wide == 2 * r + k, dest_ref[r, k].astype(F32), tag)
    packet_ref[count * elec :, :] = tag.astype(BF16)


def green_of(orbitals, dest):
    count, elec, basis = orbitals.shape
    rows = count * elec + 8
    return pl.pallas_call(
        green_kernel,
        out_shape=(jax.ShapeDtypeStruct((rows, basis), BF16), jax.ShapeDtypeStruct((8, 128), F32)),
        in_specs=[pl.BlockSpec(memory_space=pltpu.SMEM), pl.BlockSpec(memory_space=pltpu.VMEM)],
        out_specs=(pl.BlockSpec(memory_space=pltpu.VMEM), pl.BlockSpec(memory_space=pltpu.VMEM)),
        cost_estimate=pl.CostEstimate(flops=8_000_000, bytes_accessed=200_000, transcendentals=64),
        name="green",
    )(dest, orbitals)


def relayout_kernel(vectors_ref, out_ref):
    elec, group, basis = out_ref.shape
    half = group // 2
    size = half * elec
    to = iota((size, size), 0)
    of = iota((size, size), 1)
    move = ((to % half) * elec + to // half == of).astype(BF16)
    parts = []
    for h in range(2):
        moved = jnp.dot(move, vectors_ref[h * size : (h + 1) * size, :], preferred_element_type=F32)
        parts.append(moved.reshape(elec, half, basis))
    out_ref[...] = jnp.concatenate(parts, axis=1).astype(BF16)


def relayout(vectors):
    count, elec, basis = vectors.shape
    group = 16
    return pl.pallas_call(
        relayout_kernel,
        out_shape=jax.ShapeDtypeStruct((elec, count, basis), BF16),
        grid=(count // group,),
        in_specs=[pl.BlockSpec((group * elec, basis), lambda b: (b, 0))],
        out_specs=pl.BlockSpec((elec, group, basis), lambda b: (0, b, 0)),
        cost_estimate=pl.CostEstimate(
            flops=2 * count * elec * basis * 256, bytes_accessed=4 * count * elec * basis, transcendentals=0
        ),
        name="relayout",
    )(vectors.reshape(count * elec, basis))


def stop_kernel(me_ref, log_ref, *refs):
    block_refs, (vectors_ref, out_ref, green, kept, trace, cross) = refs[:4], refs[4:]
    step = pl.program_id(0)
    elec, _, walkers, count = kept.shape
    groups = 8
    per = walkers // groups
    chunk = vectors_ref.shape[0]
    basis = green.shape[1]
    me = me_ref[0]
    z, y = me // 2, me % 2

    @pl.when(step == 0)
    def _():
        size = walkers * elec
        stacked = jnp.concatenate(
            [ref[q, : per * elec, :] for ref in block_refs for q in range(2)], axis=0
        )
        to = iota((size, size), 0)
        of = iota((size, size), 1)
        j, r, c = to // walkers, (to // groups) % per, to % groups
        block = (((c // 2 + 4 - z) % 4) * 2) + ((c + y) % 2)
        move = ((block * per + r) * elec + j == of).astype(BF16)
        green[...] = jnp.dot(move, stacked, preferred_element_type=F32).astype(BF16)
        trace[...] = jnp.zeros_like(trace)
        cross[...] = jnp.zeros_like(cross)

    for ii in range(chunk):
        i = step * chunk + ii
        product = lax.dot_general(
            green[...], vectors_ref[ii], (((1,), (1,)), ((), ())), preferred_element_type=F32
        ).reshape(elec, walkers, count)
        total = jnp.zeros((walkers, count), F32)
        for j in range(elec):
            part = product[j]
            kept[j, i] = part
            total += jnp.where(j < i, part * kept[i, j], 0.0)
        same = kept[i, i]
        trace[...] += same
        cross[...] += total + 0.5 * (same * same)

    @pl.when(step == pl.num_programs(0) - 1)
    def _():
        lane = iota((groups, 128), 1)
        sub = iota((groups, 128), 0)
        tags = jnp.zeros((groups, 128), F32)
        for dz in range(4):
            for dy in range(2):
                tag = block_refs[dz][dy, per * elec :, :128].astype(F32)
                owner = ((z + dz) % 4) * 2 + (y + dy) % 2
                tags = jnp.where(sub == owner, tag, tags)
        values, wanted = [], []
        for r in range(per):
            bias = trace[r * groups : (r + 1) * groups, :]
            terms = 2.0 * (bias * bias) - 2.0 * cross[r * groups : (r + 1) * groups, :]
            energy = jnp.sum(terms, axis=1, keepdims=True)
            log = log_ref[:, r : r + 1]
            tail = jnp.where(lane == 0, 1.0, jnp.where(lane == 1, energy, 0.0))
            tail = jnp.where((lane == 2) & (sub == me), log, tail)
            values.append(jnp.concatenate([bias, tail], axis=1))
            wanted.append([tags[:, 2 * r + k : 2 * r + k + 1] for k in range(2)])
        for d in range(out_ref.shape[0] // groups):
            packet = jnp.zeros_like(values[0])
            for r in range(per):
                hit = (wanted[r][0] == float(d)) | (wanted[r][1] == float(d))
                packet = jnp.where(hit, values[r], packet)
            for c in range(groups):
                out_ref[d * groups + c] = packet[c : c + 1, :]


def stops(me, log, blocks, vectors, slots):
    elec, count, basis = vectors.shape
    walkers, chunk = 16, 4
    whole = pl.BlockSpec(memory_space=pltpu.VMEM)
    return pl.pallas_call(
        stop_kernel,
        out_shape=jax.ShapeDtypeStruct((slots, 1, count + 128), F32),
        grid=(elec // chunk,),
        in_specs=[pl.BlockSpec(memory_space=pltpu.SMEM), whole]
        + [whole] * len(blocks)
        + [pl.BlockSpec((chunk, count, basis), lambda b: (b, 0, 0))],
        out_specs=whole,
        scratch_shapes=[
            pltpu.VMEM((walkers * elec, basis), BF16),
            pltpu.VMEM((elec, elec, walkers, count), F32),
            pltpu.VMEM((walkers, count), F32),
            pltpu.VMEM((walkers, count), F32),
        ],
        cost_estimate=pl.CostEstimate(
            flops=2 * walkers * elec * elec * count * basis,
            bytes_accessed=2 * elec * count * basis,
            transcendentals=0,
        ),
        name="stops",
    )(me, log, *blocks, vectors)


def slot_kernel(scale, packets_ref, energy_ref, bias_ref, log_ref):
    slots, total = bias_ref.shape
    groups = 8
    width = packets_ref.shape[2]
    count = total // groups
    filled = jnp.zeros((groups, 1), F32)
    held = [jnp.zeros((groups, width), F32) for _ in range(slots)]
    for s in range(packets_ref.shape[0] // groups):
        packet = jnp.concatenate([packets_ref[s * groups + c] for c in range(groups)], axis=0)
        flag = packet[:, count : count + 1]
        for t in range(slots):
            held[t] = jnp.where((flag > 0.5) & (filled == float(t)), packet, held[t])
        filled = filled + flag
    for t in range(slots):
        for c in range(groups):
            bias_ref[t : t + 1, c * count : (c + 1) * count] = held[t][c : c + 1, :count]
        energy_ref[t] = jnp.sum(held[t][:, count + 1 : count + 2]) * scale
        log_ref[t] = jnp.sum(held[t][:, count + 2 : count + 3])


def slots_of(packets, slots, total, scale):
    return pl.pallas_call(
        functools.partial(slot_kernel, scale),
        out_shape=(
            jax.ShapeDtypeStruct((slots,), F32),
            jax.ShapeDtypeStruct((slots, total), F32),
            jax.ShapeDtypeStruct((slots,), F32),
        ),
        in_specs=[pl.BlockSpec(memory_space=pltpu.VMEM)],
        out_specs=(
            pl.BlockSpec(memory_space=pltpu.SMEM),
            pl.BlockSpec(memory_space=pltpu.VMEM),
            pl.BlockSpec(memory_space=pltpu.SMEM),
        ),
        name="slots",
    )(packets)


def moved(value, dz, dy):
    pairs = [
        (z * 2 + y, ((z + dz) % 4) * 2 + (y + dy) % 2) for z in range(4) for y in range(2)
    ]
    return lax.ppermute(value, "chol", pairs)


def body(orbitals, dest, chol_vectors):
    walk_count, chol_count = lax.axis_size("walk"), lax.axis_size("chol")
    walk_dev, elec, basis = orbitals.shape
    local = chol_vectors.shape[0]
    total = chol_count * local
    me = lax.axis_index("chol").astype(jnp.int32).reshape(1)
    packet, log = green_of(orbitals, dest)
    pair = jnp.stack([packet, moved(packet, 0, 1)])
    blocks = [pair, moved(pair, -1, 0), moved(pair, 2, 0), moved(pair, 1, 0)]
    vectors = relayout(chol_vectors)
    packets = stops(me, log, blocks, vectors, walk_count * chol_count)
    packets = lax.all_to_all(packets, ("walk", "chol"), split_axis=0, concat_axis=0, tiled=True)
    return slots_of(packets, 2 * walk_dev, total, 1.0 / (elec * total))


def solution(mesh):
    placed = (P(("walk", "chol"), None, None), P(("walk", "chol"), None), P("chol", None, None))
    return jax.shard_map(
        body,
        mesh=mesh,
        in_specs=placed,
        out_specs=(P(("walk", "chol")), P(("walk", "chol"), None), P(("walk", "chol"))),
        check_vma=False,
    )
```

time: 829 us -> 66.7 us (0.08); the launches traced: 814 us -> 65.9 us
  local copies, waits for them, and re-layouts: 508 us -> 0.8 us
  other arithmetic: 168 us -> 0.9 us
  waiting for transfers between devices: 60.9 us -> 1.96 us
  matrix products: 47.1 us -> 0 us
  Pallas kernels: 0 us -> 31.7 us
  blocking collectives: 0 us -> 20.3 us
  starting transfers between devices: 26.6 us -> 9.52 us
    transpose x72 -> x0, local copies, waits for them, and re-layouts: 148 us -> none  [the longest x64 148 us: one_group(): values = jnp.sum(jnp.diagonal(product, axis1=1, axis2=3), axis=2).T]
    gather x67 -> x0, local copies, waits for them, and re-layouts: 146 us -> none  [the longest x64 144 us: one_group(): values = jnp.sum(jnp.diagonal(product, axis1=1, axis2=3), axis=2).T]
    while x64 -> x0, other arithmetic: 130 us -> none
    while x78 -> x0, local copies, waits for them, and re-layouts: 120 us -> none
    dynamic_slice x64 -> x0, local copies, waits for them, and re-layouts: 83 us -> none  [stop_terms(): values, parts = lax.map(one_group, grouped)]
    dot_general x66 -> x0, matrix products: 46.3 us -> none  [the longest x64 45.6 us: one_group(): lax.dot_general(group, flat_block, (((1,), (1,)), ((), ())), preferred_el...]
    ppermute x23 -> x4, waiting for transfers between devices: 43.6 us -> 1.96 us  [moved(): return lax.ppermute(value, 'chol', pairs)]
    pallas_call x0 -> x4, Pallas kernels: none -> 31.7 us  [the longest x1 13.9 us: relayout(): pl.pallas_call(relayout_kernel, out_shape=jax.ShapeDtypeStruct((elec, cou...]
  transfers between devices with their start and end apart: 25 -> 4, of which waited for: 10 -> 1; matrix products, arithmetic and copies ran while one was open for 75% -> 0% of each run, Pallas kernels for 0% -> 21%
where the time goes in v1:
time: 66.7 us; the launch traced here: 65.9 us
  Pallas kernels  31.7 us (48%)
  blocking collectives  20.3 us (30%)
  starting transfers between devices  9.52 us (14%)
  waiting for transfers between devices  1.96 us (3%)
  other arithmetic  0.9 us (1%)
  local copies, waits for them, and re-layouts  0.8 us (1%)
  between operations  0.68 us (1%)
    all_to_all x1, blocking collectives, body(): lax.all_to_all(packets, ('walk', 'chol'), split_axis=0, concat_axis=0, ti...  20.3 us
    pallas_call x1, Pallas kernels, relayout(): pl.pallas_call(relayout_kernel, out_shape=jax.ShapeDtypeStruct((elec, cou...  13.9 us
    pallas_call x1, Pallas kernels, stops(): pl.pallas_call(stop_kernel, out_shape=jax.ShapeDtypeStruct((slots, 1, cou...  11.5 us
    ppermute x4, starting transfers between devices, moved(): return lax.ppermute(value, 'chol', pairs)  9.52 us
    pallas_call x1, Pallas kernels, green_of(): pl.pallas_call(green_kernel, out_shape=(jax.ShapeDtypeStruct((rows, basis...  4.63 us
    ppermute x4, waiting for transfers between devices, moved(): return lax.ppermute(value, 'chol', pairs)  1.96 us
    pallas_call x1, Pallas kernels, slots_of(): pl.pallas_call(functools.partial(slot_kernel, scale), out_shape=(jax.Shap...  1.79 us
  transfers between devices with their start and end apart: 4, of which 1 were waited for; matrix products, arithmetic and copies ran while one was open for 0% of the time, Pallas kernels for 21%

profile of v1, /device:TPU:1, one launch (start us, length us, event | category | flops | bytes accessed | tf_op | source)
XLA Modules:
  0.0 65.9 jit_solution(12671959739544064029)
XLA Ops:
  0.6 4.6 %green.1 = (bf16[72,512]{1,0:T(8,128)(2,1)}, f32[8,128]{1,0:T(8,128)}) custom-call(s32[2,2]{1,0:T(2,128)} %dest_ref.1, f32[2,32,512]{2,1,0:T(8,128)} %walkers_ref.1), custom_call_target="tpu_custom_call" | custom-call | flops 8000000 | bytes 200000 | tf_op jit(solution)/shard_map/green/pallas_call | solution.py:62
  5.3 3.7 %collective-permute-start = (bf16[72,512]{1,0:T(8,128)(2,1)}, bf16[72,512]{1,0:T(8,128)(2,1)S(1)}, u32[]{:S(2)}, u32[]{:S(2)}) collective-permute-start(bf16[72,512]{1,0:T(8,128)(2,1)} %get-tuple-element.6), channel_id=1, source_target_pairs={{0,1},{1,0},{2,3},{3,2},{4,5},{5,4},{6,7},{7,6},{8,9},{9,8},{10,11... | collective-permute-start | bytes 221192 | tf_op jit(solution)/shard_map/ppermute | solution.py:240
  9.0 2.0 %collective-permute-done = bf16[72,512]{1,0:T(8,128)(2,1)S(1)} collective-permute-done((bf16[72,512]{1,0:T(8,128)(2,1)}, bf16[72,512]{1,0:T(8,128)(2,1)S(1)}, u32[]{:S(2)}, u32[]{:S(2)}) %collective-permute-start) | collective-permute-done | bytes 73760 | tf_op jit(solution)/shard_map/ppermute | solution.py:240
  10.9 0.9 %pad_maximum_fusion.refs_0_ = bf16[2,72,512]{2,1,0:T(8,128)(2,1)S(1)} fusion(bf16[1,72,512]{2,1,0:T(8,128)(2,1)S(1)} %bitcast.6, bf16[1,72,512]{2,1,0:T(8,128)(2,1)} %bitcast.5), kind=kLoop, calls=%fused_computation | loop fusion | flops 73728 | bytes 294912 | tf_op jit(solution)/shard_map/stack | solution.py:250
  11.8 0.0 copy-start
  11.9 1.8 %collective-permute-start.3 = (bf16[2,72,512]{2,1,0:T(8,128)(2,1)S(1)}, bf16[2,72,512]{2,1,0:T(8,128)(2,1)S(1)}, u32[]{:S(2)}, u32[]{:S(2)}) collective-permute-start(bf16[2,72,512]{2,1,0:T(8,128)(2,1)S(1)} %pad_maximum_fusion.refs_0_), channel_id=1, source_target_pairs={{0,2},{1,3},{2,4},{3,5},{4,6},{5,7},{6,0},{7,1},{8,10},{9,11},{10,... | collective-permute-start | bytes 442376 | tf_op jit(solution)/shard_map/ppermute | solution.py:240
  13.6 3.3 %collective-permute-start.2 = (bf16[2,72,512]{2,1,0:T(8,128)(2,1)S(1)}, bf16[2,72,512]{2,1,0:T(8,128)(2,1)S(1)}, u32[]{:S(2)}, u32[]{:S(2)}) collective-permute-start(bf16[2,72,512]{2,1,0:T(8,128)(2,1)S(1)} %pad_maximum_fusion.refs_0_), channel_id=1, source_target_pairs={{0,4},{1,5},{2,6},{3,7},{4,0},{5,1},{6,2},{7,3},{8,12},{9,13},{10,... | collective-permute-start | bytes 442376 | tf_op jit(solution)/shard_map/ppermute | solution.py:240
  16.9 0.7 %collective-permute-start.1 = (bf16[2,72,512]{2,1,0:T(8,128)(2,1)S(1)}, bf16[2,72,512]{2,1,0:T(8,128)(2,1)S(1)}, u32[]{:S(2)}, u32[]{:S(2)}) collective-permute-start(bf16[2,72,512]{2,1,0:T(8,128)(2,1)S(1)} %pad_maximum_fusion.refs_0_), channel_id=1, source_target_pairs={{0,6},{1,7},{2,0},{3,1},{4,2},{5,3},{6,4},{7,5},{8,14},{9,15},{10,... | collective-permute-start | bytes 442376 | tf_op jit(solution)/shard_map/ppermute | solution.py:240
  17.6 13.9 %relayout.1.refs_4_ = bf16[32,256,512]{2,1,0:T(8,128)(2,1)} custom-call(bf16[8192,512]{1,0:T(8,128)(2,1)} %bitcast.4), custom_call_target="tpu_custom_call" | custom-call | flops 2147483648 | bytes 16777216 | tf_op jit(solution)/shard_map/relayout/pallas_call | solution.py:89
  31.5 0.0 copy-done
  31.5 0.0 collective-permute-done.3.refs_3_
  31.5 0.0 copy-start.1
  31.5 0.0 collective-permute-done.2.refs_2_
  31.5 0.0 copy-start.2
  31.6 0.0 collective-permute-done.1.refs_1_
  31.6 0.0 copy-start.3
  31.6 0.6 copy-done.1
  32.2 0.1 copy-done.2
  32.3 0.1 copy-done.3
  32.4 11.5 %stops.1 = f32[128,1,384]{2,1,0:T(1,128)} custom-call(s32[1]{0:T(128)} %bitcast.me_ref, f32[8,128]{1,0:T(8,128)} %get-tuple-element.5.log_ref, bf16[2,72,512]{2,1,0:T(8,128)(2,1)} %copy-done, bf16[2,72,512]{2,1,0:T(8,128)(2,1)} %copy-done.3, bf16[2,72,512]{2,1,0:T(8,128)(2,1)} %copy-done.2, bf16[2,72,512]{2,1,0:T(8,128)(2,1)} %copy-done.1, ...), custom_call_target="tpu_custom_call" | custom-call | flops 4294967296 | bytes 8388608 | tf_op jit(solution)/shard_map/stops/pallas_call | solution.py:175
  43.8 20.3 %all_to_all.5.packets_ref = f32[128,1,384]{2,1,0:T(1,128)} all-to-all(f32[128,1,384]{2,1,0:T(1,128)} %stops.1), channel_id=1, replica_groups=mesh['walk'=16,'chol'=8] {'walk','chol'}, dimensions={0} | all-to-all | bytes 393216 | tf_op jit(solution)/shard_map/all_to_all | solution.py:254
  64.2 1.8 %slots.1 = (f32[4]{0:T(128)}, f32[4,2048]{1,0:T(4,128)}, f32[4]{0:T(128)}) custom-call(f32[128,1,384]{2,1,0:T(1,128)} %all_to_all.5.packets_ref), custom_call_target="tpu_custom_call" | custom-call | tf_op jit(solution)/shard_map/slots/pallas_call | solution.py:219
Async XLA Ops:
  5.3 5.7 %collective-permute-start = (bf16[72,512]{1,0:T(8,128)(2,1)}, bf16[72,512]{1,0:T(8,128)(2,1)S(1)}, u32[]{:S(2)}, u32[]{:S(2)}) collective-permute-start(bf16[72,512]{1,0:T(8,128)(2,1)} %get-tuple-element.6), channel_id=1, source_target_pairs={{0,1},{1,0},{2,3},{3,2},{4,5},{5,4},{6,7},{7,6},{8,9},{9,8},{10,11... | collective-permute-start | bytes 221192 | tf_op jit(solution)/shard_map/ppermute | solution.py:240
  11.8 19.7 %copy-start = (bf16[2,72,512]{2,1,0:T(8,128)(2,1)}, bf16[2,72,512]{2,1,0:T(8,128)(2,1)S(1)}, u32[]{:S(2)}) copy-start(bf16[2,72,512]{2,1,0:T(8,128)(2,1)S(1)} %pad_maximum_fusion.refs_0_) | copy-start | bytes 442372
  11.9 19.7 %collective-permute-start.3 = (bf16[2,72,512]{2,1,0:T(8,128)(2,1)S(1)}, bf16[2,72,512]{2,1,0:T(8,128)(2,1)S(1)}, u32[]{:S(2)}, u32[]{:S(2)}) collective-permute-start(bf16[2,72,512]{2,1,0:T(8,128)(2,1)S(1)} %pad_maximum_fusion.refs_0_), channel_id=1, source_target_pairs={{0,2},{1,3},{2,4},{3,5},{4,6},{5,7},{6,0},{7,1},{8,10},{9,11},{10,... | collective-permute-start | bytes 442376 | tf_op jit(solution)/shard_map/ppermute | solution.py:240
  13.6 17.9 %collective-permute-start.2 = (bf16[2,72,512]{2,1,0:T(8,128)(2,1)S(1)}, bf16[2,72,512]{2,1,0:T(8,128)(2,1)S(1)}, u32[]{:S(2)}, u32[]{:S(2)}) collective-permute-start(bf16[2,72,512]{2,1,0:T(8,128)(2,1)S(1)} %pad_maximum_fusion.refs_0_), channel_id=1, source_target_pairs={{0,4},{1,5},{2,6},{3,7},{4,0},{5,1},{6,2},{7,3},{8,12},{9,13},{10,... | collective-permute-start | bytes 442376 | tf_op jit(solution)/shard_map/ppermute | solution.py:240
  16.9 14.6 %collective-permute-start.1 = (bf16[2,72,512]{2,1,0:T(8,128)(2,1)S(1)}, bf16[2,72,512]{2,1,0:T(8,128)(2,1)S(1)}, u32[]{:S(2)}, u32[]{:S(2)}) collective-permute-start(bf16[2,72,512]{2,1,0:T(8,128)(2,1)S(1)} %pad_maximum_fusion.refs_0_), channel_id=1, source_target_pairs={{0,6},{1,7},{2,0},{3,1},{4,2},{5,3},{6,4},{7,5},{8,14},{9,15},{10,... | collective-permute-start | bytes 442376 | tf_op jit(solution)/shard_map/ppermute | solution.py:240
  31.5 0.7 %copy-start.1 = (bf16[2,72,512]{2,1,0:T(8,128)(2,1)}, bf16[2,72,512]{2,1,0:T(8,128)(2,1)S(1)}, u32[]{:S(2)}) copy-start(bf16[2,72,512]{2,1,0:T(8,128)(2,1)S(1)} %collective-permute-done.3.refs_3_) | copy-start | bytes 442372
  31.5 0.7 %copy-start.2 = (bf16[2,72,512]{2,1,0:T(8,128)(2,1)}, bf16[2,72,512]{2,1,0:T(8,128)(2,1)S(1)}, u32[]{:S(2)}) copy-start(bf16[2,72,512]{2,1,0:T(8,128)(2,1)S(1)} %collective-permute-done.2.refs_2_) | copy-start | bytes 442372
  31.6 0.8 %copy-start.3 = (bf16[2,72,512]{2,1,0:T(8,128)(2,1)}, bf16[2,72,512]{2,1,0:T(8,128)(2,1)S(1)}, u32[]{:S(2)}) copy-start(bf16[2,72,512]{2,1,0:T(8,128)(2,1)S(1)} %collective-permute-done.1.refs_1_) | copy-start | bytes 442372

commit v2 on v1

v2 whole, which is shorter than its diff:
```python
import functools

import jax
import jax.numpy as jnp
from jax import lax
from jax.experimental import pallas as pl
from jax.experimental.pallas import tpu as pltpu
from jax.sharding import PartitionSpec as P

F32 = jnp.float32
BF16 = jnp.bfloat16
MIB = 1 << 20
HIGH = lax.Precision.HIGHEST


def iota(shape, axis):
    return lax.broadcasted_iota(jnp.int32, shape, axis)


def prepare_kernel(
    places_ref, orbitals_ref, source_ref, packet_ref, log_ref, vectors_ref, dest_ref, walkers, held, landed, arrived
):
    count, elec, basis = walkers.shape
    total = held.shape[0]
    chunks = arrived.shape[0]
    size = total // chunks
    group = 16
    half = elec // 2

    def copy(n):
        part = pl.ds(n * size, size)
        return pltpu.make_async_copy(source_ref.at[part], held.at[part], arrived.at[n])

    fetch = pltpu.make_async_copy(orbitals_ref, walkers, landed.at[0])
    fetch.start()
    read = pltpu.make_async_copy(places_ref, dest_ref, landed.at[1])
    read.start()
    for n in range(chunks):
        copy(n).start()

    rows = group * half
    to = iota((rows, rows), 0)
    of = iota((rows, rows), 1)
    move = ((to % group) * half + to // group == of).astype(BF16)

    def relayout(n):
        g, h = n // 2, n % 2
        if n % (elec // chunks) == 0:
            copy(n // (elec // chunks)).wait()
        block = held[g * group : (g + 1) * group, h * half : (h + 1) * half, :].reshape(rows, basis)
        moved = jnp.dot(move, block, preferred_element_type=F32)
        vectors_ref[h * half : (h + 1) * half, g * group : (g + 1) * group, :] = moved.reshape(
            half, group, basis
        ).astype(BF16)

    fetch.wait()
    read.wait()
    work = []
    for r in range(count):
        full = walkers[r]
        work.append(
            lax.dot_general(
                full[:, :elec], full, (((0,), (0,)), ((), ())), precision=HIGH, preferred_element_type=F32
            )
        )
    sub = iota((elec, 1), 0)
    lane = iota((1, 128), 1)
    pivots = [jnp.ones((1, 128), F32) for _ in range(count)]
    for k in range(elec):
        for r in range(count):
            a = work[r]
            row = a[k : k + 1, :]
            column = a[:, k : k + 1]
            pivot = row[:, k : k + 1]
            pivots[r] = jnp.where(lane == k, pivot, pivots[r])
            scaled = row * (1.0 / pivot)
            work[r] = jnp.where(sub == k, scaled, a - column * scaled)
        relayout(k)
    out = jnp.zeros((8, 128), F32)
    lanes = iota((8, 128), 1)
    for r in range(count):
        wanted = (dest_ref[r, 0] >= 0) | (dest_ref[r, 1] >= 0)
        packet_ref[r * elec : (r + 1) * elec, :] = jnp.where(wanted, work[r], 0.0).astype(BF16)
        log = jnp.sum(jnp.where(lane < elec, jnp.log(pivots[r]), 0.0), axis=1, keepdims=True)
        log = jnp.where(wanted, log * (0.5 / elec), 0.0)
        out = jnp.where(lanes == r, log, out)
    log_ref[...] = out
    tag = jnp.full((8, basis), -1.0, F32)
    wide = iota((8, basis), 1)
    for r in range(count):
        for k in range(2):
            tag = jnp.where(wide == 2 * r + k, dest_ref[r, k].astype(F32), tag)
    packet_ref[count * elec :, :] = tag.astype(BF16)


def prepare(dest, orbitals, vectors):
    count, elec, basis = orbitals.shape
    total = vectors.shape[0]
    chunks = 8
    rows = count * elec + 8
    hbm = pl.BlockSpec(memory_space=pltpu.HBM)
    vmem = pl.BlockSpec(memory_space=pltpu.VMEM)
    return pl.pallas_call(
        prepare_kernel,
        out_shape=(
            jax.ShapeDtypeStruct((rows, basis), BF16),
            jax.ShapeDtypeStruct((8, 128), F32),
            jax.ShapeDtypeStruct((elec, total, basis), BF16),
        ),
        in_specs=[hbm, hbm, hbm],
        out_specs=(vmem, vmem, vmem),
        scratch_shapes=[
            pltpu.SMEM(dest.shape, jnp.int32),
            pltpu.VMEM(orbitals.shape, F32),
            pltpu.VMEM(vectors.shape, BF16),
            pltpu.SemaphoreType.DMA((2,)),
            pltpu.SemaphoreType.DMA((chunks,)),
        ],
        cost_estimate=pl.CostEstimate(
            flops=2 * total * elec * basis * 256, bytes_accessed=2 * total * elec * basis, transcendentals=64
        ),
        compiler_params=pltpu.CompilerParams(vmem_limit_bytes=20 * MIB),
        name="prepare",
    )(dest, orbitals, vectors)


def stop_kernel(log_ref, *refs):
    block_refs, vector_refs, (out_ref, green, kept) = refs[:5], refs[5:-3], refs[-3:]
    elec, _, walkers, count = kept.shape
    groups = 8
    per = walkers // groups
    basis = green.shape[1]
    me = lax.axis_index("chol")
    z, y = me // 2, me % 2
    packets = [block_refs[0][...], block_refs[1][...]]
    packets += [ref[q] for ref in block_refs[2:] for q in range(2)]

    size = walkers * elec
    stacked = jnp.concatenate([packet[: per * elec] for packet in packets], axis=0)
    to = iota((size, size), 0)
    of = iota((size, size), 1)
    j, r, c = to // walkers, (to // groups) % per, to % groups
    block = (((c // 2 + 4 - z) % 4) * 2) + ((c + y) % 2)
    move = ((block * per + r) * elec + j == of).astype(BF16)
    green[...] = jnp.dot(move, stacked, preferred_element_type=F32).astype(BF16)

    trace = jnp.zeros((walkers, count), F32)
    cross = jnp.zeros((walkers, count), F32)
    for i in range(elec):
        part = i
        for ref in vector_refs:
            if part < ref.shape[0]:
                vectors = ref[part]
                break
            part -= ref.shape[0]
        product = lax.dot_general(
            green[...], vectors, (((1,), (1,)), ((), ())), preferred_element_type=F32
        ).reshape(elec, walkers, count)
        for j in range(i + 1, elec):
            kept[j, i] = product[j]
        for j in range(i):
            cross = cross + product[j] * kept[i, j]
        trace = trace + product[i]
        cross = cross + 0.5 * (product[i] * product[i])

    lane = iota((groups, 128), 1)
    sub = iota((groups, 128), 0)
    tags = jnp.zeros((groups, 128), F32)
    for dz in range(4):
        for dy in range(2):
            tag = packets[dz * 2 + dy][per * elec :, :128].astype(F32)
            owner = ((z + dz) % 4) * 2 + (y + dy) % 2
            tags = jnp.where(sub == owner, tag, tags)
    values, wanted = [], []
    for r in range(per):
        bias = trace[r * groups : (r + 1) * groups, :]
        terms = 2.0 * (bias * bias) - 2.0 * cross[r * groups : (r + 1) * groups, :]
        energy = jnp.sum(terms, axis=1, keepdims=True)
        log = log_ref[:, r : r + 1]
        tail = jnp.where(lane == 0, 1.0, jnp.where(lane == 1, energy, 0.0))
        tail = jnp.where((lane == 2) & (sub == me), log, tail)
        values.append(jnp.concatenate([bias, tail], axis=1))
        wanted.append([tags[:, 2 * r + k : 2 * r + k + 1] for k in range(2)])
    for d in range(out_ref.shape[0] // groups):
        packet = jnp.zeros_like(values[0])
        for r in range(per):
            hit = (wanted[r][0] == float(d)) | (wanted[r][1] == float(d))
            packet = jnp.where(hit, values[r], packet)
        for c in range(groups):
            out_ref[d * groups + c] = packet[c : c + 1, :]


def stops(log, blocks, vectors, slots):
    elec = sum(part.shape[0] for part in vectors)
    _, count, basis = vectors[0].shape
    walkers = 16
    whole = pl.BlockSpec(memory_space=pltpu.VMEM)
    return pl.pallas_call(
        stop_kernel,
        out_shape=jax.ShapeDtypeStruct((slots, 1, count + 128), F32),
        in_specs=[whole] + [whole] * (len(blocks) + len(vectors)),
        out_specs=whole,
        scratch_shapes=[
            pltpu.VMEM((walkers * elec, basis), BF16),
            pltpu.VMEM((elec, elec, walkers, count), F32),
        ],
        cost_estimate=pl.CostEstimate(
            flops=2 * walkers * elec * elec * count * basis,
            bytes_accessed=2 * elec * count * basis,
            transcendentals=0,
        ),
        compiler_params=pltpu.CompilerParams(vmem_limit_bytes=30 * MIB),
        name="stops",
    )(log, *blocks, *vectors)


def slot_kernel(scale, packets_ref, energy_ref, bias_ref, log_ref):
    slots, total = bias_ref.shape
    groups = 8
    width = packets_ref.shape[2]
    count = total // groups
    filled = jnp.zeros((groups, 1), F32)
    held = [jnp.zeros((groups, width), F32) for _ in range(slots)]
    for s in range(packets_ref.shape[0] // groups):
        packet = jnp.concatenate([packets_ref[s * groups + c] for c in range(groups)], axis=0)
        flag = packet[:, count : count + 1]
        for t in range(slots):
            held[t] = jnp.where((flag > 0.5) & (filled == float(t)), packet, held[t])
        filled = filled + flag
    for t in range(slots):
        for c in range(groups):
            bias_ref[t : t + 1, c * count : (c + 1) * count] = held[t][c : c + 1, :count]
        energy_ref[t] = jnp.sum(held[t][:, count + 1 : count + 2]) * scale
        log_ref[t] = jnp.sum(held[t][:, count + 2 : count + 3])


def slots_of(packets, slots, total, scale):
    return pl.pallas_call(
        functools.partial(slot_kernel, scale),
        out_shape=(
            jax.ShapeDtypeStruct((slots,), F32),
            jax.ShapeDtypeStruct((slots, total), F32),
            jax.ShapeDtypeStruct((slots,), F32),
        ),
        in_specs=[pl.BlockSpec(memory_space=pltpu.VMEM)],
        out_specs=(
            pl.BlockSpec(memory_space=pltpu.SMEM),
            pl.BlockSpec(memory_space=pltpu.VMEM),
            pl.BlockSpec(memory_space=pltpu.SMEM),
        ),
        compiler_params=pltpu.CompilerParams(vmem_limit_bytes=4 * MIB),
        name="slots",
    )(packets)


def pair_kernel(first_ref, second_ref, out_ref):
    out_ref[0] = first_ref[...]
    out_ref[1] = second_ref[...]


def paired(first, second):
    return pl.pallas_call(
        pair_kernel,
        out_shape=jax.ShapeDtypeStruct((2,) + first.shape, first.dtype),
        in_specs=[pl.BlockSpec(memory_space=pltpu.VMEM)] * 2,
        out_specs=pl.BlockSpec(memory_space=pltpu.VMEM),
        compiler_params=pltpu.CompilerParams(vmem_limit_bytes=MIB),
        name="pair",
    )(first, second)


def moved(value, dz, dy):
    pairs = [
        (z * 2 + y, ((z + dz) % 4) * 2 + (y + dy) % 2) for z in range(4) for y in range(2)
    ]
    return lax.ppermute(value, "chol", pairs)


def body(orbitals, dest, chol_vectors):
    walk_count, chol_count = lax.axis_size("walk"), lax.axis_size("chol")
    walk_dev, elec, basis = orbitals.shape
    local = chol_vectors.shape[0]
    total = chol_count * local
    dest = pltpu.with_memory_space_constraint(dest, pltpu.HBM)
    orbitals = pltpu.with_memory_space_constraint(orbitals, pltpu.HBM)
    chol_vectors = pltpu.with_memory_space_constraint(chol_vectors, pltpu.HBM)
    packet, log, vectors = prepare(dest, orbitals, chol_vectors)
    other = moved(packet, 0, 1)
    pair = paired(packet, other)
    blocks = [packet, other, moved(pair, -1, 0), moved(pair, 2, 0), moved(pair, 1, 0)]
    packets = stops(log, blocks, [vectors], walk_count * chol_count)
    packets = lax.all_to_all(packets, ("walk", "chol"), split_axis=0, concat_axis=0, tiled=True)
    return slots_of(packets, 2 * walk_dev, total, 1.0 / (elec * total))


def solution(mesh):
    placed = (P(("walk", "chol"), None, None), P(("walk", "chol"), None), P("chol", None, None))
    return jax.shard_map(
        body,
        mesh=mesh,
        in_specs=placed,
        out_specs=(P(("walk", "chol")), P(("walk", "chol"), None), P(("walk", "chol"))),
        check_vma=False,
    )
```

time: 66.7 us -> 51.1 us (0.77)
  Pallas kernels: 31.7 us -> 13.1 us
  waiting for transfers between devices: 1.96 us -> 6.26 us
  blocking collectives: 20.3 us -> 21.4 us
  other arithmetic: 0.9 us -> 0 us
  local copies, waits for them, and re-layouts: 0.8 us -> 0 us
    pallas_call x2, Pallas kernels: 18.5 us -> 6.88 us  [the longest x1 6.87 us: prepare(): pl.pallas_call(prepare_kernel, out_shape=(jax.ShapeDtypeStruct((rows, bas...]
    pallas_call x1, Pallas kernels: 11.5 us -> 5.37 us  [stops(): pl.pallas_call(stop_kernel, out_shape=jax.ShapeDtypeStruct((slots, 1, cou...]
    ppermute x4, waiting for transfers between devices: 1.96 us -> 6.26 us  [moved(): return lax.ppermute(value, 'chol', pairs)]
    all_to_all x1, blocking collectives: 20.3 us -> 21.4 us  [body(): lax.all_to_all(packets, ('walk', 'chol'), split_axis=0, concat_axis=0, ti...]
    pallas_call x1, Pallas kernels: 1.79 us -> 0.86 us  [slots_of(): pl.pallas_call(functools.partial(slot_kernel, scale), out_shape=(jax.Shap...]
    another operation x1 -> x0, other arithmetic: 0.9 us -> none  [body(): pair = jnp.stack([packet, moved(packet, 0, 1)])]
    unnamed x8 -> x0, local copies, waits for them, and re-layouts: 0.8 us -> none
  transfers between devices with their start and end apart: 4 -> 4, of which waited for: 1 -> 4; matrix products, arithmetic and copies ran while one was open for 0% -> 0% of each run, Pallas kernels for 21% -> 0%
where the time goes in v2:
time: 51.1 us; the launch traced here: 51 us
  blocking collectives  21.4 us (42%)
  Pallas kernels  13.1 us (26%)
  starting transfers between devices  9.61 us (19%)
  waiting for transfers between devices  6.26 us (12%)
  between operations  0.65 us (1%)
    all_to_all x1, blocking collectives, body(): lax.all_to_all(packets, ('walk', 'chol'), split_axis=0, concat_axis=0, ti...  21.4 us
    ppermute x4, starting transfers between devices, moved(): return lax.ppermute(value, 'chol', pairs)  9.61 us
    pallas_call x1, Pallas kernels, prepare(): pl.pallas_call(prepare_kernel, out_shape=(jax.ShapeDtypeStruct((rows, bas...  6.87 us
    ppermute x4, waiting for transfers between devices, moved(): return lax.ppermute(value, 'chol', pairs)  6.26 us
    pallas_call x1, Pallas kernels, stops(): pl.pallas_call(stop_kernel, out_shape=jax.ShapeDtypeStruct((slots, 1, cou...  5.37 us
  transfers between devices with their start and end apart: 4, of which 4 were waited for; matrix products, arithmetic and copies ran while one was open for 0% of the time, Pallas kernels for 0%

profile of v2, /device:TPU:1, one launch (start us, length us, event | category | flops | bytes accessed | tf_op | source)
XLA Modules:
  0.0 51.0 jit_solution(15127974946934645362)
XLA Ops:
  0.6 6.9 %prepare.1 = (bf16[72,512]{1,0:T(8,128)(2,1)S(1)}, f32[8,128]{1,0:T(8,128)S(1)}, bf16[32,256,512]{2,1,0:T(8,128)(2,1)S(1)}) custom-call(s32[2,2]{1,0:T(2,128)} %places_ref.1, f32[2,32,512]{2,1,0:T(8,128)} %orbitals_ref.1, bf16[256,32,512]{2,1,0:T(8,128)(2,1)} %source_ref.1), custom_call_target="tpu_custom_call" | custom-call | flops 2147483648 | bytes 8388608 | tf_op jit(solution)/shard_map/prepare/pallas_call | solution.py:103
  7.5 3.8 %collective-permute-start = (bf16[72,512]{1,0:T(8,128)(2,1)S(1)}, bf16[72,512]{1,0:T(8,128)(2,1)S(1)}, u32[]{:S(2)}, u32[]{:S(2)}) collective-permute-start(bf16[72,512]{1,0:T(8,128)(2,1)S(1)} %get-tuple-element.7.first_ref.refs_0_), channel_id=1, source_target_pairs={{0,1},{1,0},{2,3},{3,2},{4,5},{5,4},{6,7},{7,6},{8,9},{9,8},{10,11... | collective-permute-start | bytes 221192 | tf_op jit(solution)/shard_map/ppermute | solution.py:276
  11.3 1.7 %collective-permute-done.second_ref.refs_1_ = bf16[72,512]{1,0:T(8,128)(2,1)S(1)} collective-permute-done((bf16[72,512]{1,0:T(8,128)(2,1)S(1)}, bf16[72,512]{1,0:T(8,128)(2,1)S(1)}, u32[]{:S(2)}, u32[]{:S(2)}) %collective-permute-start) | collective-permute-done | bytes 73760 | tf_op jit(solution)/shard_map/ppermute | solution.py:276
  13.1 1.8 %collective-permute-start.3 = (bf16[2,72,512]{2,1,0:T(8,128)(2,1)S(1)}, bf16[2,72,512]{2,1,0:T(8,128)(2,1)S(1)}, u32[]{:S(2)}, u32[]{:S(2)}) collective-permute-start(bf16[2,72,512]{2,1,0:T(8,128)(2,1)S(1)} %pair.1), channel_id=1, source_target_pairs={{0,2},{1,3},{2,4},{3,5},{4,6},{5,7},{6,0},{7,1},{8,10},{9,11},{10,... | collective-permute-start | bytes 442376 | tf_op jit(solution)/shard_map/ppermute | solution.py:276
  14.8 3.3 %collective-permute-start.2 = (bf16[2,72,512]{2,1,0:T(8,128)(2,1)S(1)}, bf16[2,72,512]{2,1,0:T(8,128)(2,1)S(1)}, u32[]{:S(2)}, u32[]{:S(2)}) collective-permute-start(bf16[2,72,512]{2,1,0:T(8,128)(2,1)S(1)} %pair.1), channel_id=1, source_target_pairs={{0,4},{1,5},{2,6},{3,7},{4,0},{5,1},{6,2},{7,3},{8,12},{9,13},{10,... | collective-permute-start | bytes 442376 | tf_op jit(solution)/shard_map/ppermute | solution.py:276
  18.1 0.7 %collective-permute-start.1 = (bf16[2,72,512]{2,1,0:T(8,128)(2,1)S(1)}, bf16[2,72,512]{2,1,0:T(8,128)(2,1)S(1)}, u32[]{:S(2)}, u32[]{:S(2)}) collective-permute-start(bf16[2,72,512]{2,1,0:T(8,128)(2,1)S(1)} %pair.1), channel_id=1, source_target_pairs={{0,6},{1,7},{2,0},{3,1},{4,2},{5,3},{6,4},{7,5},{8,14},{9,15},{10,... | collective-permute-start | bytes 442376 | tf_op jit(solution)/shard_map/ppermute | solution.py:276
  18.9 0.6 %collective-permute-done.3.refs_4_ = bf16[2,72,512]{2,1,0:T(8,128)(2,1)S(1)} collective-permute-done((bf16[2,72,512]{2,1,0:T(8,128)(2,1)S(1)}, bf16[2,72,512]{2,1,0:T(8,128)(2,1)S(1)}, u32[]{:S(2)}, u32[]{:S(2)}) %collective-permute-start.3) | collective-permute-done | bytes 147488 | tf_op jit(solution)/shard_map/ppermute | solution.py:276
  19.5 3.6 %collective-permute-done.2.refs_3_ = bf16[2,72,512]{2,1,0:T(8,128)(2,1)S(1)} collective-permute-done((bf16[2,72,512]{2,1,0:T(8,128)(2,1)S(1)}, bf16[2,72,512]{2,1,0:T(8,128)(2,1)S(1)}, u32[]{:S(2)}, u32[]{:S(2)}) %collective-permute-start.2) | collective-permute-done | bytes 147488 | tf_op jit(solution)/shard_map/ppermute | solution.py:276
  23.1 0.3 collective-permute-done.1.refs_2_
  23.4 5.4 %stops.1 = f32[128,1,384]{2,1,0:T(1,128)S(1)} custom-call(f32[8,128]{1,0:T(8,128)S(1)} %get-tuple-element.6.log_ref, bf16[72,512]{1,0:T(8,128)(2,1)S(1)} %get-tuple-element.7.first_ref.refs_0_, bf16[72,512]{1,0:T(8,128)(2,1)S(1)} %collective-permute-done.second_ref.refs_1_, bf16[2,72,512]{2,1,0:T(8,128)(2,1)S(1)} %collective-permute-done.1.refs_2_, ...), custom_call_target="tpu_custom_call" | custom-call | flops 4294967296 | bytes 8388608 | tf_op jit(solution)/shard_map/stops/pallas_call | solution.py:198
  28.8 21.4 %all_to_all.5.packets_ref = f32[128,1,384]{2,1,0:T(1,128)S(1)} all-to-all(f32[128,1,384]{2,1,0:T(1,128)S(1)} %stops.1), channel_id=1, replica_groups=mesh['walk'=16,'chol'=8] {'walk','chol'}, dimensions={0} | all-to-all | bytes 393216 | tf_op jit(solution)/shard_map/all_to_all | solution.py:292
  50.1 0.9 %slots.1 = (f32[4]{0:T(128)}, f32[4,2048]{1,0:T(4,128)}, f32[4]{0:T(128)}) custom-call(f32[128,1,384]{2,1,0:T(1,128)S(1)} %all_to_all.5.packets_ref), custom_call_target="tpu_custom_call" | custom-call | tf_op jit(solution)/shard_map/slots/pallas_call | solution.py:238
  (1 shorter events, 0.0 us)
Async XLA Ops:
  7.5 5.6 %collective-permute-start = (bf16[72,512]{1,0:T(8,128)(2,1)S(1)}, bf16[72,512]{1,0:T(8,128)(2,1)S(1)}, u32[]{:S(2)}, u32[]{:S(2)}) collective-permute-start(bf16[72,512]{1,0:T(8,128)(2,1)S(1)} %get-tuple-element.7.first_ref.refs_0_), channel_id=1, source_target_pairs={{0,1},{1,0},{2,3},{3,2},{4,5},{5,4},{6,7},{7,6},{8,9},{9,8},{10,11... | collective-permute-start | bytes 221192 | tf_op jit(solution)/shard_map/ppermute | solution.py:276
  13.1 6.4 %collective-permute-start.3 = (bf16[2,72,512]{2,1,0:T(8,128)(2,1)S(1)}, bf16[2,72,512]{2,1,0:T(8,128)(2,1)S(1)}, u32[]{:S(2)}, u32[]{:S(2)}) collective-permute-start(bf16[2,72,512]{2,1,0:T(8,128)(2,1)S(1)} %pair.1), channel_id=1, source_target_pairs={{0,2},{1,3},{2,4},{3,5},{4,6},{5,7},{6,0},{7,1},{8,10},{9,11},{10,... | collective-permute-start | bytes 442376 | tf_op jit(solution)/shard_map/ppermute | solution.py:276
  14.8 8.3 %collective-permute-start.2 = (bf16[2,72,512]{2,1,0:T(8,128)(2,1)S(1)}, bf16[2,72,512]{2,1,0:T(8,128)(2,1)S(1)}, u32[]{:S(2)}, u32[]{:S(2)}) collective-permute-start(bf16[2,72,512]{2,1,0:T(8,128)(2,1)S(1)} %pair.1), channel_id=1, source_target_pairs={{0,4},{1,5},{2,6},{3,7},{4,0},{5,1},{6,2},{7,3},{8,12},{9,13},{10,... | collective-permute-start | bytes 442376 | tf_op jit(solution)/shard_map/ppermute | solution.py:276
  18.1 5.3 %collective-permute-start.1 = (bf16[2,72,512]{2,1,0:T(8,128)(2,1)S(1)}, bf16[2,72,512]{2,1,0:T(8,128)(2,1)S(1)}, u32[]{:S(2)}, u32[]{:S(2)}) collective-permute-start(bf16[2,72,512]{2,1,0:T(8,128)(2,1)S(1)} %pair.1), channel_id=1, source_target_pairs={{0,6},{1,7},{2,0},{3,1},{4,2},{5,3},{6,4},{7,5},{8,14},{9,15},{10,... | collective-permute-start | bytes 442376 | tf_op jit(solution)/shard_map/ppermute | solution.py:276

commit v3 on v2

v3 whole, which is shorter than its diff:
```python
import functools

import jax
import jax.numpy as jnp
from jax import lax
from jax.experimental import pallas as pl
from jax.experimental.pallas import tpu as pltpu
from jax.sharding import PartitionSpec as P

F32 = jnp.float32
BF16 = jnp.bfloat16
MIB = 1 << 20
HIGH = lax.Precision.HIGHEST


def iota(shape, axis):
    return lax.broadcasted_iota(jnp.int32, shape, axis)


def green_kernel(places_ref, orbitals_ref, packet_ref, log_ref, dest_ref, walkers, landed):
    count, elec, basis = walkers.shape
    fetch = pltpu.make_async_copy(orbitals_ref, walkers, landed.at[0])
    fetch.start()
    read = pltpu.make_async_copy(places_ref, dest_ref, landed.at[1])
    read.start()
    fetch.wait()
    read.wait()
    work = []
    for r in range(count):
        full = walkers[r]
        work.append(
            lax.dot_general(
                full[:, :elec], full, (((0,), (0,)), ((), ())), precision=HIGH, preferred_element_type=F32
            )
        )
    sub = iota((elec, 1), 0)
    lane = iota((1, 128), 1)
    pivots = [jnp.ones((1, 128), F32) for _ in range(count)]
    for k in range(elec):
        for r in range(count):
            a = work[r]
            row = a[k : k + 1, :]
            column = a[:, k : k + 1]
            pivot = row[:, k : k + 1]
            pivots[r] = jnp.where(lane == k, pivot, pivots[r])
            scaled = row * (1.0 / pivot)
            work[r] = jnp.where(sub == k, scaled, a - column * scaled)
    out = jnp.zeros((8, 128), F32)
    lanes = iota((8, 128), 1)
    for r in range(count):
        wanted = (dest_ref[r, 0] >= 0) | (dest_ref[r, 1] >= 0)
        packet_ref[r * elec : (r + 1) * elec, :] = jnp.where(wanted, work[r], 0.0).astype(BF16)
        log = jnp.sum(jnp.where(lane < elec, jnp.log(pivots[r]), 0.0), axis=1, keepdims=True)
        log = jnp.where(wanted, log * (0.5 / elec), 0.0)
        out = jnp.where(lanes == r, log, out)
    log_ref[...] = out
    tag = jnp.full((8, basis), -1.0, F32)
    wide = iota((8, basis), 1)
    for r in range(count):
        for k in range(2):
            tag = jnp.where(wide == 2 * r + k, dest_ref[r, k].astype(F32), tag)
    packet_ref[count * elec :, :] = tag.astype(BF16)


def green_of(dest, orbitals):
    count, elec, basis = orbitals.shape
    rows = count * elec + 8
    hbm = pl.BlockSpec(memory_space=pltpu.HBM)
    vmem = pl.BlockSpec(memory_space=pltpu.VMEM)
    return pl.pallas_call(
        green_kernel,
        out_shape=(jax.ShapeDtypeStruct((rows, basis), BF16), jax.ShapeDtypeStruct((8, 128), F32)),
        in_specs=[hbm, hbm],
        out_specs=(vmem, vmem),
        scratch_shapes=[
            pltpu.SMEM(dest.shape, jnp.int32),
            pltpu.VMEM(orbitals.shape, F32),
            pltpu.SemaphoreType.DMA((2,)),
        ],
        cost_estimate=pl.CostEstimate(flops=8_000_000, bytes_accessed=200_000, transcendentals=64),
        compiler_params=pltpu.CompilerParams(vmem_limit_bytes=4 * MIB),
        name="green",
    )(dest, orbitals)


def relayout_kernel(first, vectors_ref, out_ref, held, arrived):
    elec, count, basis = out_ref.shape
    chunks = arrived.shape[0]
    size = count // chunks
    group = 16

    def copy(n):
        part = pl.ds(n * size, size)
        return pltpu.make_async_copy(
            vectors_ref.at[part, pl.ds(first, elec), :], held.at[part], arrived.at[n]
        )

    for n in range(chunks):
        copy(n).start()
    rows = group * elec
    to = iota((rows, rows), 0)
    of = iota((rows, rows), 1)
    move = ((to % group) * elec + to // group == of).astype(BF16)
    for n in range(chunks):
        copy(n).wait()
        for b in range(n * size // group, (n + 1) * size // group):
            block = held[b * group : (b + 1) * group].reshape(rows, basis)
            moved = jnp.dot(move, block, preferred_element_type=F32)
            out_ref[:, b * group : (b + 1) * group, :] = moved.reshape(elec, group, basis).astype(BF16)


def relayout(vectors, first, elec):
    count, _, basis = vectors.shape
    chunks = 8
    return pl.pallas_call(
        functools.partial(relayout_kernel, first),
        out_shape=jax.ShapeDtypeStruct((elec, count, basis), BF16),
        in_specs=[pl.BlockSpec(memory_space=pltpu.HBM)],
        out_specs=pl.BlockSpec(memory_space=pltpu.VMEM),
        scratch_shapes=[pltpu.VMEM((count, elec, basis), BF16), pltpu.SemaphoreType.DMA((chunks,))],
        cost_estimate=pl.CostEstimate(
            flops=2 * count * elec * basis * 256, bytes_accessed=2 * count * elec * basis, transcendentals=0
        ),
        compiler_params=pltpu.CompilerParams(vmem_limit_bytes=10 * MIB),
    )(vectors)


def sums_of(blocks, vector_refs, kept):
    elec, _, walkers, count = kept.shape
    per = walkers // len(blocks)
    size = walkers * elec
    stacked = jnp.concatenate([block[: per * elec] for block in blocks], axis=0)
    to = iota((size, size), 0)
    of = iota((size, size), 1)
    j, r, q = to // walkers, (to // len(blocks)) % per, to % len(blocks)
    move = ((q * per + r) * elec + j == of).astype(BF16)
    green = jnp.dot(move, stacked, preferred_element_type=F32).astype(BF16)
    trace = jnp.zeros((walkers, count), F32)
    cross = jnp.zeros((walkers, count), F32)
    for i in range(elec):
        ref = vector_refs[i * len(vector_refs) // elec]
        product = lax.dot_general(
            green, ref[i % ref.shape[0]], (((1,), (1,)), ((), ())), preferred_element_type=F32
        ).reshape(elec, walkers, count)
        for j in range(i + 1, elec):
            kept[j, i] = product[j]
        for j in range(i):
            cross = cross + product[j] * kept[i, j]
        trace = trace + product[i]
        cross = cross + 0.5 * (product[i] * product[i])
    return trace, cross


def values_of(trace, cross):
    lane = iota((trace.shape[0], 128), 1)
    terms = 2.0 * (trace * trace) - 2.0 * cross
    energy = jnp.sum(terms, axis=1, keepdims=True)
    tail = jnp.where(lane == 0, 1.0, jnp.where(lane == 1, energy, 0.0))
    return jnp.concatenate([trace, tail], axis=1)


def first_kernel(own_ref, other_ref, pair_ref, *refs):
    vector_refs, (out_ref, kept) = refs[:-2], refs[-2:]
    blocks = [own_ref[...], other_ref[...], pair_ref[0], pair_ref[1]]
    out_ref[...] = values_of(*sums_of(blocks, vector_refs, kept))


def second_kernel(log_ref, early_ref, own_ref, other_ref, near_ref, far_ref, back_ref, *refs):
    vector_refs, (out_ref, kept) = refs[:-2], refs[-2:]
    groups = 8
    blocks = [far_ref[0], far_ref[1], back_ref[0], back_ref[1]]
    late = values_of(*sums_of(blocks, vector_refs, kept))
    early = early_ref[...]
    width = early.shape[1]
    row = iota((groups, width), 0)
    lane = iota((groups, width), 1)
    for r in range(2):
        here = (row == 4 * r) & (lane == width - 126)
        early = jnp.where(here, log_ref[:, r : r + 1], early)
    me = lax.axis_index("chol")
    z, y = me // 2, me % 2
    values = [early, late]
    blocks = [[own_ref[...], other_ref[...], near_ref[0], near_ref[1]], blocks]
    rows = blocks[0][0].shape[0] - 8
    short = iota((groups, 128), 0)
    for h in range(2):
        tags = jnp.zeros((groups, 128), F32)
        for q in range(4):
            tags = jnp.where(short % 4 == q, blocks[h][q][rows:, :128].astype(F32), tags)
        wanted = [
            jnp.where(iota((groups, 1), 0) < 4, tags[:, k : k + 1], tags[:, 2 + k : 3 + k]) for k in range(2)
        ]
        owners = [((z + 2 * h + q // 2) % 4) * 2 + (y + q) % 2 for q in range(4)]
        for d in range(out_ref.shape[0] // groups):
            hit = (wanted[0] == float(d)) | (wanted[1] == float(d))
            packet = jnp.where(hit, values[h], 0.0)
            packet = packet[:4] + packet[4:]
            for q in range(4):
                out_ref[d * groups + owners[q]] = packet[q : q + 1, :]


def stops(kernel, shape, operands, vectors):
    elec = sum(part.shape[0] for part in vectors)
    _, count, basis = vectors[0].shape
    walkers = 8
    whole = pl.BlockSpec(memory_space=pltpu.VMEM)
    return pl.pallas_call(
        kernel,
        out_shape=jax.ShapeDtypeStruct(shape, F32),
        in_specs=[whole] * (len(operands) + len(vectors)),
        out_specs=whole,
        scratch_shapes=[pltpu.VMEM((elec, elec, walkers, count), F32)],
        cost_estimate=pl.CostEstimate(
            flops=2 * walkers * elec * elec * count * basis,
            bytes_accessed=2 * elec * count * basis,
            transcendentals=0,
        ),
        compiler_params=pltpu.CompilerParams(vmem_limit_bytes=16 * MIB),
    )(*operands, *vectors)


def slot_kernel(scale, packets_ref, energy_ref, bias_ref, log_ref):
    slots, total = bias_ref.shape
    groups = 8
    width = packets_ref.shape[2]
    count = total // groups
    filled = jnp.zeros((groups, 1), F32)
    held = [jnp.zeros((groups, width), F32) for _ in range(slots)]
    for s in range(packets_ref.shape[0] // groups):
        packet = jnp.concatenate([packets_ref[s * groups + c] for c in range(groups)], axis=0)
        flag = packet[:, count : count + 1]
        for t in range(slots):
            held[t] = jnp.where((flag > 0.5) & (filled == float(t)), packet, held[t])
        filled = filled + flag
    for t in range(slots):
        for c in range(groups):
            bias_ref[t : t + 1, c * count : (c + 1) * count] = held[t][c : c + 1, :count]
        energy_ref[t] = jnp.sum(held[t][:, count + 1 : count + 2]) * scale
        log_ref[t] = jnp.sum(held[t][:, count + 2 : count + 3])


def slots_of(packets, slots, total, scale):
    return pl.pallas_call(
        functools.partial(slot_kernel, scale),
        out_shape=(
            jax.ShapeDtypeStruct((slots,), F32),
            jax.ShapeDtypeStruct((slots, total), F32),
            jax.ShapeDtypeStruct((slots,), F32),
        ),
        in_specs=[pl.BlockSpec(memory_space=pltpu.VMEM)],
        out_specs=(
            pl.BlockSpec(memory_space=pltpu.SMEM),
            pl.BlockSpec(memory_space=pltpu.VMEM),
            pl.BlockSpec(memory_space=pltpu.SMEM),
        ),
        compiler_params=pltpu.CompilerParams(vmem_limit_bytes=4 * MIB),
        name="slots",
    )(packets)


def pair_kernel(first_ref, second_ref, out_ref):
    out_ref[0] = first_ref[...]
    out_ref[1] = second_ref[...]


def paired(first, second):
    return pl.pallas_call(
        pair_kernel,
        out_shape=jax.ShapeDtypeStruct((2,) + first.shape, first.dtype),
        in_specs=[pl.BlockSpec(memory_space=pltpu.VMEM)] * 2,
        out_specs=pl.BlockSpec(memory_space=pltpu.VMEM),
        compiler_params=pltpu.CompilerParams(vmem_limit_bytes=MIB),
        name="pair",
    )(first, second)


def moved(value, dz, dy):
    pairs = [
        (z * 2 + y, ((z + dz) % 4) * 2 + (y + dy) % 2) for z in range(4) for y in range(2)
    ]
    return lax.ppermute(value, "chol", pairs)


def body(orbitals, dest, chol_vectors):
    walk_count, chol_count = lax.axis_size("walk"), lax.axis_size("chol")
    walk_dev, elec, _ = orbitals.shape
    local = chol_vectors.shape[0]
    total = chol_count * local
    width = local + 128
    dest = pltpu.with_memory_space_constraint(dest, pltpu.HBM)
    orbitals = pltpu.with_memory_space_constraint(orbitals, pltpu.HBM)
    chol_vectors = pltpu.with_memory_space_constraint(chol_vectors, pltpu.HBM)
    packet, log = green_of(dest, orbitals)
    other = moved(packet, 0, 1)
    pair = paired(packet, other)
    near = moved(pair, -1, 0)
    far = moved(pair, 2, 0)
    back = moved(pair, 1, 0)
    lower = relayout(chol_vectors, 0, elec // 2)
    upper = relayout(chol_vectors, elec // 2, elec // 2)
    vectors = [lower, upper]
    early = stops(first_kernel, (8, width), [packet, other, near], vectors)
    packets = stops(
        second_kernel,
        (walk_count * chol_count, 1, width),
        [log, early, packet, other, near, far, back],
        vectors,
    )
    packets = lax.all_to_all(packets, ("walk", "chol"), split_axis=0, concat_axis=0, tiled=True)
    return slots_of(packets, 2 * walk_dev, total, 1.0 / (elec * total))


def solution(mesh):
    placed = (P(("walk", "chol"), None, None), P(("walk", "chol"), None), P("chol", None, None))
    return jax.shard_map(
        body,
        mesh=mesh,
        in_specs=placed,
        out_specs=(P(("walk", "chol")), P(("walk", "chol"), None), P(("walk", "chol"))),
        check_vma=False,
    )
```

time: 51.1 us -> 53.3 us (1.043)
  Pallas kernels: 13.1 us -> 17.2 us
  blocking collectives: 21.4 us -> 19.2 us
  waiting for transfers between devices: 6.26 us -> 7.01 us
  starting transfers between devices: 9.61 us -> 9.06 us
    pallas_call x2 -> x5, Pallas kernels: 12.2 us -> 16.3 us  [the longest x2 7.07 us: relayout(): pl.pallas_call(functools.partial(relayout_kernel, first), out_shape=jax.S...]
    all_to_all x1, blocking collectives: 21.4 us -> 19.2 us  [body(): lax.all_to_all(packets, ('walk', 'chol'), split_axis=0, concat_axis=0, ti...]
    ppermute x4, waiting for transfers between devices: 6.26 us -> 7.01 us  [moved(): return lax.ppermute(value, 'chol', pairs)]
    ppermute x4, starting transfers between devices: 9.61 us -> 9.06 us  [moved(): return lax.ppermute(value, 'chol', pairs)]
  transfers between devices with their start and end apart: 4 -> 4, of which waited for: 4 -> 2; matrix products, arithmetic and copies ran while one was open for 0% -> 0% of each run, Pallas kernels for 0% -> 18%
where the time goes in v3:
time: 53.3 us; the launch traced here: 53.1 us
  blocking collectives  19.2 us (36%)
  Pallas kernels  17.2 us (32%)
  starting transfers between devices  9.06 us (17%)
  waiting for transfers between devices  7.01 us (13%)
  between operations  0.68 us (1%)
    all_to_all x1, blocking collectives, body(): lax.all_to_all(packets, ('walk', 'chol'), split_axis=0, concat_axis=0, ti...  19.2 us
    ppermute x4, starting transfers between devices, moved(): return lax.ppermute(value, 'chol', pairs)  9.06 us
    pallas_call x2, Pallas kernels, relayout(): pl.pallas_call(functools.partial(relayout_kernel, first), out_shape=jax.S...  7.07 us
    ppermute x4, waiting for transfers between devices, moved(): return lax.ppermute(value, 'chol', pairs)  7.01 us
    pallas_call x2, Pallas kernels, stops(): pl.pallas_call(kernel, out_shape=jax.ShapeDtypeStruct(shape, F32), in_spe...  5.23 us
    pallas_call x1, Pallas kernels, green_of(): pl.pallas_call(green_kernel, out_shape=(jax.ShapeDtypeStruct((rows, basis...  4.02 us
  transfers between devices with their start and end apart: 4, of which 2 were waited for; matrix products, arithmetic and copies ran while one was open for 0% of the time, Pallas kernels for 18%

profile of v3, /device:TPU:1, one launch (start us, length us, event | category | flops | bytes accessed | tf_op | source)
XLA Modules:
  0.0 53.1 jit_solution(970301856785907132)
XLA Ops:
  0.6 4.0 %green.1 = (bf16[72,512]{1,0:T(8,128)(2,1)S(1)}, f32[8,128]{1,0:T(8,128)S(1)}) custom-call(s32[2,2]{1,0:T(2,128)} %places_ref.1, f32[2,32,512]{2,1,0:T(8,128)} %orbitals_ref.1), custom_call_target="tpu_custom_call" | custom-call | flops 8000000 | bytes 200000 | tf_op jit(solution)/shard_map/green/pallas_call | solution.py:70
  4.7 3.8 %collective-permute-start = (bf16[72,512]{1,0:T(8,128)(2,1)S(1)}, bf16[72,512]{1,0:T(8,128)(2,1)S(1)}, u32[]{:S(2)}, u32[]{:S(2)}) collective-permute-start(bf16[72,512]{1,0:T(8,128)(2,1)S(1)} %get-tuple-element.6.first_ref.own_ref), channel_id=1, source_target_pairs={{0,1},{1,0},{2,3},{3,2},{4,5},{5,4},{6,7},{7,6},{8,9},{9,8},{10,11... | collective-permute-start | bytes 221192 | tf_op jit(solution)/shard_map/ppermute | solution.py:281
  8.5 1.7 %collective-permute-done.second_ref.other_ref = bf16[72,512]{1,0:T(8,128)(2,1)S(1)} collective-permute-done((bf16[72,512]{1,0:T(8,128)(2,1)S(1)}, bf16[72,512]{1,0:T(8,128)(2,1)S(1)}, u32[]{:S(2)}, u32[]{:S(2)}) %collective-permute-start) | collective-permute-done | bytes 73760 | tf_op jit(solution)/shard_map/ppermute | solution.py:281
  10.2 3.9 %collective-permute-start.1 = (bf16[2,72,512]{2,1,0:T(8,128)(2,1)S(1)}, bf16[2,72,512]{2,1,0:T(8,128)(2,1)S(1)}, u32[]{:S(2)}, u32[]{:S(2)}) collective-permute-start(bf16[2,72,512]{2,1,0:T(8,128)(2,1)S(1)} %pair.1), channel_id=1, source_target_pairs={{0,6},{1,7},{2,0},{3,1},{4,2},{5,3},{6,4},{7,5},{8,14},{9,15},{10,... | collective-permute-start | bytes 442376 | tf_op jit(solution)/shard_map/ppermute | solution.py:281
  14.1 3.5 %shard_map.59.refs_1_ = bf16[16,256,512]{2,1,0:T(8,128)(2,1)S(1)} custom-call(bf16[256,32,512]{2,1,0:T(8,128)(2,1)} %vectors_ref.3), custom_call_target="tpu_custom_call" | custom-call | flops 1073741824 | bytes 4194304 | tf_op jit(solution)/shard_map/pallas_call | solution.py:115
  17.6 3.5 %shard_map.58.refs_0_ = bf16[16,256,512]{2,1,0:T(8,128)(2,1)S(1)} custom-call(bf16[256,32,512]{2,1,0:T(8,128)(2,1)} %vectors_ref.3), custom_call_target="tpu_custom_call" | custom-call | flops 1073741824 | bytes 4194304 | tf_op jit(solution)/shard_map/pallas_call | solution.py:115
  21.2 0.1 collective-permute-start.3
  21.3 1.3 %collective-permute-start.2 = (bf16[2,72,512]{2,1,0:T(8,128)(2,1)S(1)}, bf16[2,72,512]{2,1,0:T(8,128)(2,1)S(1)}, u32[]{:S(2)}, u32[]{:S(2)}) collective-permute-start(bf16[2,72,512]{2,1,0:T(8,128)(2,1)S(1)} %pair.1), channel_id=1, source_target_pairs={{0,4},{1,5},{2,6},{3,7},{4,0},{5,1},{6,2},{7,3},{8,12},{9,13},{10,... | collective-permute-start | bytes 442376 | tf_op jit(solution)/shard_map/ppermute | solution.py:281
  22.6 0.0 collective-permute-done.1.pair_ref.near_ref
  22.6 2.6 %shard_map.60.early_ref = f32[8,384]{1,0:T(8,128)S(1)} custom-call(bf16[72,512]{1,0:T(8,128)(2,1)S(1)} %get-tuple-element.6.first_ref.own_ref, bf16[72,512]{1,0:T(8,128)(2,1)S(1)} %collective-permute-done.second_ref.other_ref, bf16[2,72,512]{2,1,0:T(8,128)(2,1)S(1)} %collective-permute-done.1.pair_ref.near_ref, bf16[16,256,512]{2,1,0:T(8,128)(2,1)S(1)} %shard_map.58.refs_0_, ...), custom_call_target="tpu_custom_call" | custom-call | flops 2147483648 | bytes 8388608 | tf_op jit(solution)/shard_map/pallas_call | solution.py:207
  25.2 5.3 %collective-permute-done.3.back_ref = bf16[2,72,512]{2,1,0:T(8,128)(2,1)S(1)} collective-permute-done((bf16[2,72,512]{2,1,0:T(8,128)(2,1)S(1)}, bf16[2,72,512]{2,1,0:T(8,128)(2,1)S(1)}, u32[]{:S(2)}, u32[]{:S(2)}) %collective-permute-start.3) | collective-permute-done | bytes 147488 | tf_op jit(solution)/shard_map/ppermute | solution.py:281
  30.4 0.0 collective-permute-done.2.far_ref
  30.4 2.6 %shard_map.61 = f32[128,1,384]{2,1,0:T(1,128)S(1)} custom-call(f32[8,128]{1,0:T(8,128)S(1)} %get-tuple-element.5.log_ref, f32[8,384]{1,0:T(8,128)S(1)} %shard_map.60.early_ref, bf16[72,512]{1,0:T(8,128)(2,1)S(1)} %get-tuple-element.6.first_ref.own_ref, bf16[72,512]{1,0:T(8,128)(2,1)S(1)} %collective-permute-done.second_ref.other_ref, ...), custom_call_target="tpu_custom_call" | custom-call | flops 2147483648 | bytes 8388608 | tf_op jit(solution)/shard_map/pallas_call | solution.py:207
  33.1 19.2 %all_to_all.5.packets_ref = f32[128,1,384]{2,1,0:T(1,128)S(1)} all-to-all(f32[128,1,384]{2,1,0:T(1,128)S(1)} %shard_map.61), channel_id=1, replica_groups=mesh['walk'=16,'chol'=8] {'walk','chol'}, dimensions={0} | all-to-all | bytes 393216 | tf_op jit(solution)/shard_map/all_to_all | solution.py:309
  52.2 0.9 %slots.1 = (f32[4]{0:T(128)}, f32[4,2048]{1,0:T(4,128)}, f32[4]{0:T(128)}) custom-call(f32[128,1,384]{2,1,0:T(1,128)S(1)} %all_to_all.5.packets_ref), custom_call_target="tpu_custom_call" | custom-call | tf_op jit(solution)/shard_map/slots/pallas_call | solution.py:243
  (1 shorter events, 0.0 us)
Async XLA Ops:
  4.7 5.6 %collective-permute-start = (bf16[72,512]{1,0:T(8,128)(2,1)S(1)}, bf16[72,512]{1,0:T(8,128)(2,1)S(1)}, u32[]{:S(2)}, u32[]{:S(2)}) collective-permute-start(bf16[72,512]{1,0:T(8,128)(2,1)S(1)} %get-tuple-element.6.first_ref.own_ref), channel_id=1, source_target_pairs={{0,1},{1,0},{2,3},{3,2},{4,5},{5,4},{6,7},{7,6},{8,9},{9,8},{10,11... | collective-permute-start | bytes 221192 | tf_op jit(solution)/shard_map/ppermute | solution.py:281
  10.2 12.3 %collective-permute-start.1 = (bf16[2,72,512]{2,1,0:T(8,128)(2,1)S(1)}, bf16[2,72,512]{2,1,0:T(8,128)(2,1)S(1)}, u32[]{:S(2)}, u32[]{:S(2)}) collective-permute-start(bf16[2,72,512]{2,1,0:T(8,128)(2,1)S(1)} %pair.1), channel_id=1, source_target_pairs={{0,6},{1,7},{2,0},{3,1},{4,2},{5,3},{6,4},{7,5},{8,14},{9,15},{10,... | collective-permute-start | bytes 442376 | tf_op jit(solution)/shard_map/ppermute | solution.py:281
  21.2 9.2 %collective-permute-start.3 = (bf16[2,72,512]{2,1,0:T(8,128)(2,1)S(1)}, bf16[2,72,512]{2,1,0:T(8,128)(2,1)S(1)}, u32[]{:S(2)}, u32[]{:S(2)}) collective-permute-start(bf16[2,72,512]{2,1,0:T(8,128)(2,1)S(1)} %pair.1), channel_id=1, source_target_pairs={{0,2},{1,3},{2,4},{3,5},{4,6},{5,7},{6,0},{7,1},{8,10},{9,11},{10,... | collective-permute-start | bytes 442376 | tf_op jit(solution)/shard_map/ppermute | solution.py:281
  21.3 9.2 %collective-permute-start.2 = (bf16[2,72,512]{2,1,0:T(8,128)(2,1)S(1)}, bf16[2,72,512]{2,1,0:T(8,128)(2,1)S(1)}, u32[]{:S(2)}, u32[]{:S(2)}) collective-permute-start(bf16[2,72,512]{2,1,0:T(8,128)(2,1)S(1)} %pair.1), channel_id=1, source_target_pairs={{0,4},{1,5},{2,6},{3,7},{4,0},{5,1},{6,2},{7,3},{8,12},{9,13},{10,... | collective-permute-start | bytes 442376 | tf_op jit(solution)/shard_map/ppermute | solution.py:281

commit v4 on v3

--- a/solution.py
+++ b/solution.py
@@ -17,74 +17,111 @@
     return lax.broadcasted_iota(jnp.int32, shape, axis)
 
 
-def green_kernel(places_ref, orbitals_ref, packet_ref, log_ref, dest_ref, walkers, landed):
-    count, elec, basis = walkers.shape
+def normal_rows(walkers):
+    elec, basis = walkers.shape
+    whole = lax.dot_general(
+        walkers[:, :elec], walkers, (((0,), (0,)), ((), ())), precision=HIGH, preferred_element_type=F32
+    )
+    return [[whole[n : n + 8, t : t + 128] for t in range(0, basis, 128)] for n in range(0, elec, 8)]
+
+
+def eliminate(parts, pivots, k):
+    home, at = k // 8, k % 8
+    sub = iota((8, 128), 0)
+    lane = iota((1, 128), 1)
+    upper = [tile[at : at + 1] for tile in parts[home]]
+    lower = [tile[at + 1 : at + 2] for tile in parts[home]]
+
+    def spread(tile, n):
+        return jnp.broadcast_to(tile[:, n : n + 1], tile.shape)
+
+    left = [spread(part[0], k) for part in parts]
+    right = [spread(part[0], k + 1) for part in parts]
+    pivot, below = spread(upper[0], k), spread(lower[0], k)
+    inverse = 1.0 / pivot
+    link = spread(upper[0], k + 1) * inverse
+    after = spread(lower[0], k + 1) - below * link
+    inverse_after = 1.0 / after
+    tops = [tile * inverse for tile in upper]
+    bottoms = [(tile - below * top) * inverse_after for tile, top in zip(lower, tops)]
+    uppers = [top - link * bottom for top, bottom in zip(tops, bottoms)]
+    right = [b - a * link for a, b in zip(left, right)]
+    pivots = jnp.where(lane == k, pivot, jnp.where(lane == k + 1, after, pivots))
+    out = []
+    for n, part in enumerate(parts):
+        tiles = []
+        for tile, top, bottom, first in zip(part, tops, bottoms, uppers):
+            new = (tile - left[n] * top) - right[n] * bottom
+            if n == home:
+                new = jnp.where(sub == at, first, jnp.where(sub == at + 1, bottom, new))
+            tiles.append(new)
+        out.append(tiles)
+    return out, pivots
+
+
+def green_kernel(
+    places_ref, orbitals_ref, vectors_ref, packet_ref, log_ref, raw_ref, dest_ref, walkers, landed, arrived
+):
+    count, elec, _ = walkers.shape
     fetch = pltpu.make_async_copy(orbitals_ref, walkers, landed.at[0])
     fetch.start()
     read = pltpu.make_async_copy(places_ref, dest_ref, landed.at[1])
     read.start()
+    ahead = pltpu.make_async_copy(vectors_ref.at[:, pl.ds(0, raw_ref.shape[1]), :], raw_ref, arrived)
+    ahead.start()
     fetch.wait()
     read.wait()
-    work = []
-    for r in range(count):
-        full = walkers[r]
-        work.append(
-            lax.dot_general(
-                full[:, :elec], full, (((0,), (0,)), ((), ())), precision=HIGH, preferred_element_type=F32
-            )
-        )
-    sub = iota((elec, 1), 0)
+    pivots = [jnp.ones((1, 128), F32) for _ in range(count)]
+    parts = [normal_rows(walkers[r]) for r in range(count)]
+    for k in range(0, elec, 2):
+        for r in range(count):
+            parts[r], pivots[r] = eliminate(parts[r], pivots[r], k)
+    out = jnp.zeros((8, 128), F32)
     lane = iota((1, 128), 1)
-    pivots = [jnp.ones((1, 128), F32) for _ in range(count)]
-    for k in range(elec):
-        for r in range(count):
-            a = work[r]
-            row = a[k : k + 1, :]
-            column = a[:, k : k + 1]
-            pivot = row[:, k : k + 1]
-            pivots[r] = jnp.where(lane == k, pivot, pivots[r])
-            scaled = row * (1.0 / pivot)
-            work[r] = jnp.where(sub == k, scaled, a - column * scaled)
-    out = jnp.zeros((8, 128), F32)
     lanes = iota((8, 128), 1)
     for r in range(count):
         wanted = (dest_ref[r, 0] >= 0) | (dest_ref[r, 1] >= 0)
-        packet_ref[r * elec : (r + 1) * elec, :] = jnp.where(wanted, work[r], 0.0).astype(BF16)
+        green = jnp.where(wanted, jnp.concatenate([jnp.concatenate(part, axis=1) for part in parts[r]], axis=0), 0.0)
+        tag = jnp.where(
+            lane == 0, dest_ref[r, 0].astype(F32), jnp.where(lane == 1, dest_ref[r, 1].astype(F32), 0.0)
+        )
+        rows = slice(r * elec, (r + 1) * elec)
+        packet_ref[rows, :128] = jnp.where(lane < elec, tag, green[:, :128]).astype(BF16)
+        packet_ref[rows, 128:] = green[:, 128:].astype(BF16)
         log = jnp.sum(jnp.where(lane < elec, jnp.log(pivots[r]), 0.0), axis=1, keepdims=True)
         log = jnp.where(wanted, log * (0.5 / elec), 0.0)
         out = jnp.where(lanes == r, log, out)
     log_ref[...] = out
-    tag = jnp.full((8, basis), -1.0, F32)
-    wide = iota((8, basis), 1)
-    for r in range(count):
-        for k in range(2):
-            tag = jnp.where(wide == 2 * r + k, dest_ref[r, k].astype(F32), tag)
-    packet_ref[count * elec :, :] = tag.astype(BF16)
-
-
-def green_of(dest, orbitals):
+    ahead.wait()
+
+
+def green_of(dest, orbitals, vectors):
     count, elec, basis = orbitals.shape
-    rows = count * elec + 8
     hbm = pl.BlockSpec(memory_space=pltpu.HBM)
     vmem = pl.BlockSpec(memory_space=pltpu.VMEM)
     return pl.pallas_call(
         green_kernel,
-        out_shape=(jax.ShapeDtypeStruct((rows, basis), BF16), jax.ShapeDtypeStruct((8, 128), F32)),
-        in_specs=[hbm, hbm],
-        out_specs=(vmem, vmem),
+        out_shape=(
+            jax.ShapeDtypeStruct((count * elec, basis), BF16),
+            jax.ShapeDtypeStruct((8, 128), F32),
+            jax.ShapeDtypeStruct((vectors.shape[0], elec // 2, basis), BF16),
+        ),
+        in_specs=[hbm, hbm, hbm],
+        out_specs=(vmem, vmem, vmem),
         scratch_shapes=[
             pltpu.SMEM(dest.shape, jnp.int32),
             pltpu.VMEM(orbitals.shape, F32),
             pltpu.SemaphoreType.DMA((2,)),
+            pltpu.SemaphoreType.DMA,
         ],
-        cost_estimate=pl.CostEstimate(flops=8_000_000, bytes_accessed=200_000, transcendentals=64),
+        cost_estimate=pl.CostEstimate(flops=8_000_000, bytes_accessed=4_400_000, transcendentals=64),
         compiler_params=pltpu.CompilerParams(vmem_limit_bytes=4 * MIB),
         name="green",
-    )(dest, orbitals)
-
-
-def relayout_kernel(first, vectors_ref, out_ref, held, arrived):
-    elec, count, basis = out_ref.shape
+    )(dest, orbitals, vectors)
+
+
+def relayout_kernel(raw_ref, vectors_ref, out_ref, held, arrived):
+    count, half, basis = held.shape
     chunks = arrived.shape[0]
     size = count // chunks
     group = 16
@@ -92,49 +129,56 @@
     def copy(n):
         part = pl.ds(n * size, size)
         return pltpu.make_async_copy(
-            vectors_ref.at[part, pl.ds(first, elec), :], held.at[part], arrived.at[n]
+            vectors_ref.at[part, pl.ds(half, half), :], held.at[part], arrived.at[n]
         )
 
     for n in range(chunks):
         copy(n).start()
-    rows = group * elec
+    rows = group * half
     to = iota((rows, rows), 0)
     of = iota((rows, rows), 1)
-    move = ((to % group) * elec + to // group == of).astype(BF16)
-    for n in range(chunks):
-        copy(n).wait()
-        for b in range(n * size // group, (n + 1) * size // group):
-            block = held[b * group : (b + 1) * group].reshape(rows, basis)
-            moved = jnp.dot(move, block, preferred_element_type=F32)
-            out_ref[:, b * group : (b + 1) * group, :] = moved.reshape(elec, group, basis).astype(BF16)
-
-
-def relayout(vectors, first, elec):
-    count, _, basis = vectors.shape
-    chunks = 8
-    return pl.pallas_call(
-        functools.partial(relayout_kernel, first),
+    move = ((to % group) * half + to // group == of).astype(BF16)
+    for h, ref in enumerate((raw_ref, held)):
+        for n in range(chunks):
+            if h:
+                copy(n).wait()
+            for b in range(n * size // group, (n + 1) * size // group):
+                part = slice(b * group, (b + 1) * group)
+                moved = jnp.dot(move, ref[part].reshape(rows, basis), preferred_element_type=F32)
+                out_ref[h * half : (h + 1) * half, part, :] = moved.reshape(half, group, basis).astype(BF16)
+
+
+def relayout(raw, vectors):
+    count, elec, basis = vectors.shape
+    chunks = 4
+    vmem = pl.BlockSpec(memory_space=pltpu.VMEM)
+    return pl.pallas_call(
+        relayout_kernel,
         out_shape=jax.ShapeDtypeStruct((elec, count, basis), BF16),
-        in_specs=[pl.BlockSpec(memory_space=pltpu.HBM)],
-        out_specs=pl.BlockSpec(memory_space=pltpu.VMEM),
-        scratch_shapes=[pltpu.VMEM((count, elec, basis), BF16), pltpu.SemaphoreType.DMA((chunks,))],
+        in_specs=[vmem, pl.BlockSpec(memory_space=pltpu.HBM)],
+        out_specs=vmem,
+        scratch_shapes=[pltpu.VMEM(raw.shape, BF16), pltpu.SemaphoreType.DMA((chunks,))],
         cost_estimate=pl.CostEstimate(
             flops=2 * count * elec * basis * 256, bytes_accessed=2 * count * elec * basis, transcendentals=0
         ),
         compiler_params=pltpu.CompilerParams(vmem_limit_bytes=10 * MIB),
-    )(vectors)
+        name="relayout",
+    )(raw, vectors)
 
 
 def sums_of(blocks, vector_refs, kept):
     elec, _, walkers, count = kept.shape
     per = walkers // len(blocks)
     size = walkers * elec
-    stacked = jnp.concatenate([block[: per * elec] for block in blocks], axis=0)
+    stacked = jnp.concatenate(blocks, axis=0)
     to = iota((size, size), 0)
     of = iota((size, size), 1)
     j, r, q = to // walkers, (to // len(blocks)) % per, to % len(blocks)
     move = ((q * per + r) * elec + j == of).astype(BF16)
-    green = jnp.dot(move, stacked, preferred_element_type=F32).astype(BF16)
+    green = jnp.dot(move, stacked, preferred_element_type=F32)
+    row, lane = iota((size, 128), 0), iota((size, 128), 1)
+    head = jnp.where(lane < elec, (lane == row // walkers).astype(F32), green[:, :128])
+    green = jnp.concatenate([head, green[:, 128:]], axis=1).astype(BF16)
     trace = jnp.zeros((walkers, count), F32)
     cross = jnp.zeros((walkers, count), F32)
     for i in range(elec):
@@ -181,15 +225,15 @@
     z, y = me // 2, me % 2
     values = [early, late]
     blocks = [[own_ref[...], other_ref[...], near_ref[0], near_ref[1]], blocks]
-    rows = blocks[0][0].shape[0] - 8
+    rows = blocks[0][0].shape[0] // 2
     short = iota((groups, 128), 0)
     for h in range(2):
         tags = jnp.zeros((groups, 128), F32)
-        for q in range(4):
-            tags = jnp.where(short % 4 == q, blocks[h][q][rows:, :128].astype(F32), tags)
-        wanted = [
-            jnp.where(iota((groups, 1), 0) < 4, tags[:, k : k + 1], tags[:, 2 + k : 3 + k]) for k in range(2)
-        ]
+        for r in range(2):
+            for q in range(4):
+                tag = blocks[h][q][r * rows : r * rows + 16, :128].astype(F32)[:groups]
+                tags = jnp.where(short == 4 * r + q, tag, tags)
+        wanted = [tags[:, k : k + 1] for k in range(2)]
         owners = [((z + 2 * h + q // 2) % 4) * 2 + (y + q) % 2 for q in range(4)]
         for d in range(out_ref.shape[0] // groups):
             hit = (wanted[0] == float(d)) | (wanted[1] == float(d))
@@ -290,21 +334,16 @@
     dest = pltpu.with_memory_space_constraint(dest, pltpu.HBM)
     orbitals = pltpu.with_memory_space_constraint(orbitals, pltpu.HBM)
     chol_vectors = pltpu.with_memory_space_constraint(chol_vectors, pltpu.HBM)
-    packet, log = green_of(dest, orbitals)
+    packet, log, raw = green_of(dest, orbitals, chol_vectors)
     other = moved(packet, 0, 1)
     pair = paired(packet, other)
     near = moved(pair, -1, 0)
     far = moved(pair, 2, 0)
     back = moved(pair, 1, 0)
-    lower = relayout(chol_vectors, 0, elec // 2)
-    upper = relayout(chol_vectors, elec // 2, elec // 2)
-    vectors = [lower, upper]
+    vectors = [relayout(raw, chol_vectors)]
     early = stops(first_kernel, (8, width), [packet, other, near], vectors)
     packets = stops(
-        second_kernel,
-        (walk_count * chol_count, 1, width),
-        [log, early, packet, other, near, far, back],
-        vectors,
+        second_kernel, (walk_count * chol_count, 1, width), [log, early, packet, other, near, far, back], vectors
     )
     packets = lax.all_to_all(packets, ("walk", "chol"), split_axis=0, concat_axis=0, tiled=True)
     return slots_of(packets, 2 * walk_dev, total, 1.0 / (elec * total))

time: 53.3 us -> 47.1 us (0.88)
  Pallas kernels: 17.2 us -> 12.2 us
  waiting for transfers between devices: 7.01 us -> 5.73 us
  blocking collectives: 19.2 us -> 19.9 us
  starting transfers between devices: 9.06 us -> 8.46 us
    pallas_call x3 -> x2, Pallas kernels: 11.1 us -> 6.14 us  [the longest x1 3.08 us: green_of(): pl.pallas_call(green_kernel, out_shape=(jax.ShapeDtypeStruct((count * ele...]
    ppermute x4, waiting for transfers between devices: 7.01 us -> 5.73 us  [moved(): return lax.ppermute(value, 'chol', pairs)]
    all_to_all x1, blocking collectives: 19.2 us -> 19.9 us  [body(): lax.all_to_all(packets, ('walk', 'chol'), split_axis=0, concat_axis=0, ti...]
    ppermute x4, starting transfers between devices: 9.06 us -> 8.46 us  [moved(): return lax.ppermute(value, 'chol', pairs)]
  transfers between devices with their start and end apart: 4 -> 4, of which waited for: 2 -> 3; matrix products, arithmetic and copies ran while one was open for 0% -> 0% of each run, Pallas kernels for 18% -> 12%
where the time goes in v4:
time: 47.1 us; the launch traced here: 46.9 us
  blocking collectives  19.9 us (42%)
  Pallas kernels  12.2 us (26%)
  starting transfers between devices  8.46 us (18%)
  waiting for transfers between devices  5.73 us (12%)
  between operations  0.67 us (1%)
    all_to_all x1, blocking collectives, body(): lax.all_to_all(packets, ('walk', 'chol'), split_axis=0, concat_axis=0, ti...  19.9 us
    ppermute x4, starting transfers between devices, moved(): return lax.ppermute(value, 'chol', pairs)  8.46 us
    ppermute x4, waiting for transfers between devices, moved(): return lax.ppermute(value, 'chol', pairs)  5.73 us
    pallas_call x2, Pallas kernels, stops(): pl.pallas_call(kernel, out_shape=jax.ShapeDtypeStruct(shape, F32), in_spe...  5.21 us
    pallas_call x1, Pallas kernels, green_of(): pl.pallas_call(green_kernel, out_shape=(jax.ShapeDtypeStruct((count * ele...  3.08 us
    pallas_call x1, Pallas kernels, relayout(): pl.pallas_call(relayout_kernel, out_shape=jax.ShapeDtypeStruct((elec, cou...  3.06 us
  transfers between devices with their start and end apart: 4, of which 3 were waited for; matrix products, arithmetic and copies ran while one was open for 0% of the time, Pallas kernels for 12%

profile of v4, /device:TPU:1, one launch (start us, length us, event | category | flops | bytes accessed | tf_op | source)
XLA Modules:
  0.0 46.9 jit_solution(15075547992677421691)
XLA Ops:
  0.6 3.1 %green.1 = (bf16[64,512]{1,0:T(8,128)(2,1)S(1)}, f32[8,128]{1,0:T(8,128)S(1)}, bf16[256,16,512]{2,1,0:T(8,128)(2,1)S(1)}) custom-call(s32[2,2]{1,0:T(2,128)} %places_ref.1, f32[2,32,512]{2,1,0:T(8,128)} %orbitals_ref.1, bf16[256,32,512]{2,1,0:T(8,128)(2,1)} %vectors_ref.3), custom_call_target="tpu_custom_call" | custom-call | flops 8000000 | bytes 4400000 | tf_op jit(solution)/shard_map/green/pallas_call | solution.py:102
  3.7 3.8 %collective-permute-start = (bf16[64,512]{1,0:T(8,128)(2,1)S(1)}, bf16[64,512]{1,0:T(8,128)(2,1)S(1)}, u32[]{:S(2)}, u32[]{:S(2)}) collective-permute-start(bf16[64,512]{1,0:T(8,128)(2,1)S(1)} %get-tuple-element.7.first_ref.own_ref), channel_id=1, source_target_pairs={{0,1},{1,0},{2,3},{3,2},{4,5},{5,4},{6,7},{7,6},{8,9},{9,8},{10,11... | collective-permute-start | bytes 196616 | tf_op jit(solution)/shard_map/ppermute | solution.py:325
  7.5 1.7 %collective-permute-done.second_ref.other_ref = bf16[64,512]{1,0:T(8,128)(2,1)S(1)} collective-permute-done((bf16[64,512]{1,0:T(8,128)(2,1)S(1)}, bf16[64,512]{1,0:T(8,128)(2,1)S(1)}, u32[]{:S(2)}, u32[]{:S(2)}) %collective-permute-start) | collective-permute-done | bytes 65568 | tf_op jit(solution)/shard_map/ppermute | solution.py:325
  9.2 3.9 %collective-permute-start.1 = (bf16[2,64,512]{2,1,0:T(8,128)(2,1)S(1)}, bf16[2,64,512]{2,1,0:T(8,128)(2,1)S(1)}, u32[]{:S(2)}, u32[]{:S(2)}) collective-permute-start(bf16[2,64,512]{2,1,0:T(8,128)(2,1)S(1)} %pair.1), channel_id=1, source_target_pairs={{0,6},{1,7},{2,0},{3,1},{4,2},{5,3},{6,4},{7,5},{8,14},{9,15},{10,... | collective-permute-start | bytes 393224 | tf_op jit(solution)/shard_map/ppermute | solution.py:325
  13.1 3.1 %relayout.1.refs_0_ = bf16[32,256,512]{2,1,0:T(8,128)(2,1)S(1)} custom-call(bf16[256,16,512]{2,1,0:T(8,128)(2,1)S(1)} %get-tuple-element.8.raw_ref, bf16[256,32,512]{2,1,0:T(8,128)(2,1)} %vectors_ref.3), custom_call_target="tpu_custom_call" | custom-call | flops 2147483648 | bytes 8388608 | tf_op jit(solution)/shard_map/relayout/pallas_call | solution.py:155
  16.1 0.1 collective-permute-start.2
  16.2 0.7 %collective-permute-start.3 = (bf16[2,64,512]{2,1,0:T(8,128)(2,1)S(1)}, bf16[2,64,512]{2,1,0:T(8,128)(2,1)S(1)}, u32[]{:S(2)}, u32[]{:S(2)}) collective-permute-start(bf16[2,64,512]{2,1,0:T(8,128)(2,1)S(1)} %pair.1), channel_id=1, source_target_pairs={{0,2},{1,3},{2,4},{3,5},{4,6},{5,7},{6,0},{7,1},{8,10},{9,11},{10,... | collective-permute-start | bytes 393224 | tf_op jit(solution)/shard_map/ppermute | solution.py:325
  16.9 0.0 collective-permute-done.1.pair_ref.near_ref
  16.9 2.6 %shard_map.58.early_ref = f32[8,384]{1,0:T(8,128)S(1)} custom-call(bf16[64,512]{1,0:T(8,128)(2,1)S(1)} %get-tuple-element.7.first_ref.own_ref, bf16[64,512]{1,0:T(8,128)(2,1)S(1)} %collective-permute-done.second_ref.other_ref, bf16[2,64,512]{2,1,0:T(8,128)(2,1)S(1)} %collective-permute-done.1.pair_ref.near_ref, bf16[32,256,512]{2,1,0:T(8,128)(2,1)S(1)} %relayout.1.refs_0_), custom_call_target="tpu_custom_call" | custom-call | flops 2147483648 | bytes 8388608 | tf_op jit(solution)/shard_map/pallas_call | solution.py:251
  19.5 2.1 %collective-permute-done.2.far_ref = bf16[2,64,512]{2,1,0:T(8,128)(2,1)S(1)} collective-permute-done((bf16[2,64,512]{2,1,0:T(8,128)(2,1)S(1)}, bf16[2,64,512]{2,1,0:T(8,128)(2,1)S(1)}, u32[]{:S(2)}, u32[]{:S(2)}) %collective-permute-start.2) | collective-permute-done | bytes 131104 | tf_op jit(solution)/shard_map/ppermute | solution.py:325
  21.7 1.9 %collective-permute-done.3.back_ref = bf16[2,64,512]{2,1,0:T(8,128)(2,1)S(1)} collective-permute-done((bf16[2,64,512]{2,1,0:T(8,128)(2,1)S(1)}, bf16[2,64,512]{2,1,0:T(8,128)(2,1)S(1)}, u32[]{:S(2)}, u32[]{:S(2)}) %collective-permute-start.3) | collective-permute-done | bytes 131104 | tf_op jit(solution)/shard_map/ppermute | solution.py:325
  23.6 2.6 %shard_map.59 = f32[128,1,384]{2,1,0:T(1,128)S(1)} custom-call(f32[8,128]{1,0:T(8,128)S(1)} %get-tuple-element.6.log_ref, f32[8,384]{1,0:T(8,128)S(1)} %shard_map.58.early_ref, bf16[64,512]{1,0:T(8,128)(2,1)S(1)} %get-tuple-element.7.first_ref.own_ref, bf16[64,512]{1,0:T(8,128)(2,1)S(1)} %collective-permute-done.second_ref.other_ref, ...), custom_call_target="tpu_custom_call" | custom-call | flops 2147483648 | bytes 8388608 | tf_op jit(solution)/shard_map/pallas_call | solution.py:251
  26.2 19.9 %all_to_all.5.packets_ref = f32[128,1,384]{2,1,0:T(1,128)S(1)} all-to-all(f32[128,1,384]{2,1,0:T(1,128)S(1)} %shard_map.59), channel_id=1, replica_groups=mesh['walk'=16,'chol'=8] {'walk','chol'}, dimensions={0} | all-to-all | bytes 393216 | tf_op jit(solution)/shard_map/all_to_all | solution.py:348
  46.1 0.9 %slots.1 = (f32[4]{0:T(128)}, f32[4,2048]{1,0:T(4,128)}, f32[4]{0:T(128)}) custom-call(f32[128,1,384]{2,1,0:T(1,128)S(1)} %all_to_all.5.packets_ref), custom_call_target="tpu_custom_call" | custom-call | tf_op jit(solution)/shard_map/slots/pallas_call | solution.py:287
  (1 shorter events, 0.0 us)
Async XLA Ops:
  3.7 5.5 %collective-permute-start = (bf16[64,512]{1,0:T(8,128)(2,1)S(1)}, bf16[64,512]{1,0:T(8,128)(2,1)S(1)}, u32[]{:S(2)}, u32[]{:S(2)}) collective-permute-start(bf16[64,512]{1,0:T(8,128)(2,1)S(1)} %get-tuple-element.7.first_ref.own_ref), channel_id=1, source_target_pairs={{0,1},{1,0},{2,3},{3,2},{4,5},{5,4},{6,7},{7,6},{8,9},{9,8},{10,11... | collective-permute-start | bytes 196616 | tf_op jit(solution)/shard_map/ppermute | solution.py:325
  9.2 7.7 %collective-permute-start.1 = (bf16[2,64,512]{2,1,0:T(8,128)(2,1)S(1)}, bf16[2,64,512]{2,1,0:T(8,128)(2,1)S(1)}, u32[]{:S(2)}, u32[]{:S(2)}) collective-permute-start(bf16[2,64,512]{2,1,0:T(8,128)(2,1)S(1)} %pair.1), channel_id=1, source_target_pairs={{0,6},{1,7},{2,0},{3,1},{4,2},{5,3},{6,4},{7,5},{8,14},{9,15},{10,... | collective-permute-start | bytes 393224 | tf_op jit(solution)/shard_map/ppermute | solution.py:325
  16.1 5.5 %collective-permute-start.2 = (bf16[2,64,512]{2,1,0:T(8,128)(2,1)S(1)}, bf16[2,64,512]{2,1,0:T(8,128)(2,1)S(1)}, u32[]{:S(2)}, u32[]{:S(2)}) collective-permute-start(bf16[2,64,512]{2,1,0:T(8,128)(2,1)S(1)} %pair.1), channel_id=1, source_target_pairs={{0,4},{1,5},{2,6},{3,7},{4,0},{5,1},{6,2},{7,3},{8,12},{9,13},{10,... | collective-permute-start | bytes 393224 | tf_op jit(solution)/shard_map/ppermute | solution.py:325
  16.2 7.3 %collective-permute-start.3 = (bf16[2,64,512]{2,1,0:T(8,128)(2,1)S(1)}, bf16[2,64,512]{2,1,0:T(8,128)(2,1)S(1)}, u32[]{:S(2)}, u32[]{:S(2)}) collective-permute-start(bf16[2,64,512]{2,1,0:T(8,128)(2,1)S(1)} %pair.1), channel_id=1, source_target_pairs={{0,2},{1,3},{2,4},{3,5},{4,6},{5,7},{6,0},{7,1},{8,10},{9,11},{10,... | collective-permute-start | bytes 393224 | tf_op jit(solution)/shard_map/ppermute | solution.py:325
